TPU v7x, 768 devices: a whole 4x8x12 slice. The times are simulated.
768 devices in a mesh: segment: 32 (over z_lo, y), mp: 24 (over z_hi, x, core).
Axes of the slice: x: 4, y: 8, z: 12 (z_hi: 3, z_lo: 4; z = z_hi * 4 + z_lo), core: 2. Of those that a mesh axis runs over, the one named last changes fastest.
Arguments:
- enc_out: bfloat16 [2, 192, 4096], P(None, 'mp', 'segment'), may hold values from -6 to 6
- dec_in: bfloat16 [2, 32, 512, 4096], P(None, 'segment'), may hold values from -43 to 43
- grad_context: bfloat16 [2, 32, 512, 3072], P(None, 'segment', None, 'mp'), may hold values from -6 to 6
- w_query: bfloat16 [32, 4096, 3072], P('segment', None, 'mp'), may hold values from -0.09375 to 0.09375
- w_keyval: bfloat16 [32, 4096, 2, 3072], P('segment', None, None, 'mp'), may hold values from -0.09375 to 0.09375
- src_len: int32 [2], replicated, may hold values from 48 to 192, as said below
Outputs:
- context: bfloat16 [2, 32, 512, 3072], P(None, 'segment', None, 'mp')
- d_enc: float32 [2, 192, 4096], P(None, 'mp', 'segment')
Inputs may be any that keep to these rules, and one draw needn't show every extreme that they name: `src_len`: one micro-batch is unpadded.
All inputs are finite; a program needn't handle non-finite values.
Results may differ from a plain program's by a relative error of at most 0.017.
The roundings to bfloat16 on the way count: a program that leaves them out, or rounds other values in their place, can miss the bound.
Values may be sent and summed in bfloat16 or wider, within the bound.
A program may use at most 64 MiB of HBM per device.

v0:
```python
import math

import jax
import jax.numpy as jnp
from jax import lax
from jax.sharding import PartitionSpec as P

HD = 64


def attend_pass(query, keyval, cotangent, usable):
    num_batch, num_tgt, width = query.shape
    num_heads = width // HD
    inv_root = 1.0 / math.sqrt(HD)
    query_heads = query.reshape(num_batch, num_tgt, num_heads, HD)
    key_heads = keyval[:, :, 0].reshape(num_batch, -1, num_heads, HD)
    value_heads = keyval[:, :, 1].reshape(num_batch, -1, num_heads, HD)
    cot_heads = cotangent.reshape(num_batch, num_tgt, num_heads, HD)
    scores = (
        jnp.einsum("bthe,bshe->bhts", query_heads, key_heads, preferred_element_type=jnp.float32)
        * inv_root
    )
    scores = jnp.where(usable[:, None, None, :], scores, jnp.float32(-1e30))
    shifted = scores - jnp.max(scores, axis=-1, keepdims=True)
    raised = jnp.exp(shifted)
    attend = raised / jnp.sum(raised, axis=-1, keepdims=True)
    attend_low = attend.astype(jnp.bfloat16)
    context = jnp.einsum(
        "bhts,bshe->bthe", attend_low, value_heads, preferred_element_type=jnp.float32
    ).astype(jnp.bfloat16)
    slope = jnp.einsum(
        "bthe,bshe->bhts", cot_heads, value_heads, preferred_element_type=jnp.float32
    )
    row_dot = jnp.einsum("bthe,bthe->bht", cot_heads, context, preferred_element_type=jnp.float32)
    dscore = (attend * (slope - row_dot[..., None]) * inv_root).astype(jnp.bfloat16)
    dkey = jnp.einsum(
        "bhts,bthe->bshe", dscore, query_heads, preferred_element_type=jnp.float32
    ).astype(jnp.bfloat16)
    dvalue = jnp.einsum(
        "bhts,bthe->bshe", attend_low, cot_heads, preferred_element_type=jnp.float32
    ).astype(jnp.bfloat16)
    dkeyval = jnp.stack(
        [dkey.reshape(num_batch, -1, width), dvalue.reshape(num_batch, -1, width)], axis=2
    )
    return (context.reshape(num_batch, num_tgt, width), dkeyval)


def local(enc_out, dec_in, grad_context, w_query, w_keyval, src_len):
    inputs = dec_in[:, 0]
    cotangent = grad_context[:, 0]
    query_w = w_query[0]
    keyval_w = w_keyval[0]
    query = jnp.einsum("btd,dh->bth", inputs, query_w, preferred_element_type=jnp.float32).astype(
        jnp.bfloat16
    )
    features = lax.all_gather(enc_out, "segment", axis=2, tiled=True)
    keyval = jnp.einsum(
        "bsd,dch->bsch",
        lax.all_gather(features, "mp", axis=1, tiled=True),
        keyval_w,
        preferred_element_type=jnp.float32,
    ).astype(jnp.bfloat16)
    total_src = keyval.shape[1]
    usable = jnp.arange(total_src)[None, :] < src_len[:, None]
    context, dkeyval = attend_pass(query, keyval, cotangent, usable)
    layer_grad = jnp.einsum("bsch,dch->bsd", dkeyval, keyval_w, preferred_element_type=jnp.float32)
    by_heads = lax.psum_scatter(layer_grad, "mp", scatter_dimension=1, tiled=True)
    d_enc = lax.psum_scatter(by_heads, "segment", scatter_dimension=2, tiled=True)
    return (context[:, None], d_enc)


def solution(mesh):
    placed = (
        P(None, "mp", "segment"),
        P(None, "segment", None, None),
        P(None, "segment", None, "mp"),
        P("segment", None, "mp"),
        P("segment", None, None, "mp"),
        P(),
    )
    return jax.shard_map(
        local,
        mesh=mesh,
        in_specs=placed,
        out_specs=(P(None, "segment", None, "mp"), P(None, "mp", "segment")),
        check_vma=False,
    )
```

profile of v0, /device:TPU:6, one launch (start us, length us, event | category | flops | bytes accessed | tf_op | source)
XLA Modules:
  0.0 536.0 jit_solution(7839256769191362242)
XLA Ops:
  7.2 0.0 copy-start
  7.2 0.0 all-gather.2.cloned.1.call-start
  7.2 87.5 %all_gather.6 = bf16[2,8,4096]{2,1,0:T(8,128)(2,1)} all-gather(bf16[2,8,128]{2,1,0:T(8,128)(2,1)} %param.6), channel_id=1, replica_groups=mesh['segment'=32,'mp'=24] {'segment'}, dimensions={2}, use_global_device_ids=true | all-gather | bytes 135168 | tf_op jit(solution)/shard_map/all_gather | solution.py:56
  94.8 0.0 all-gather.2.cloned.1.call-update
  94.8 0.0 reduce-scatter.3.cloned.1.call-start
  94.8 1.1 copy.21
  95.9 0.7 iota_compare_fusion
  96.7 0.0 copy-done
  96.7 0.0 copy-start.1
  96.7 7.1 %fusion.14 = bf16[2,512,128]{1,2,0:T(8,128)(2,1)} fusion(bf16[2,1,512,4096]{3,2,1,0:T(8,128)(2,1)} %param.7, bf16[1,4096,128]{2,1,0:T(8,128)(2,1)S(1)} %copy-done), kind=kOutput, calls=%fused_computation.17 | convolution fusion | flops 1073872896 | bytes 9699328 | tf_op jit(solution)/shard_map/btd,dh->bth/dot_general | solution.py:53
  103.8 73.1 %all-gather.2.cloned.1.call-done = bf16[2,192,4096]{2,1,0:T(8,128)(2,1)} async-done(((bf16[2,8,4096]{2,1,0:T(8,128)(2,1)}), bf16[2,192,4096]{2,1,0:T(8,128)(2,1)}) %all-gather.2.cloned.1.call-update) | async-done | bytes 3145744 | tf_op jit(solution)/shard_map/all_gather | solution.py:59
  177.0 0.0 copy-done.1
  177.0 2.9 fusion.17
  179.8 0.6 fusion.36
  180.5 1.7 copy.20
  182.1 0.8 copy.18
  182.9 2.8 fusion.37
  185.7 0.0 copy-start.3
  185.7 1.6 fusion.26
  187.3 0.4 convolution_convert_fusion.1
  187.7 0.0 copy-done.3
  187.7 1.0 fusion.27
  188.7 2.9 fusion.22
  191.6 1.0 copy.22
  192.6 0.1 copy.23
  192.7 3.7 convolution_bitcast_fusion
  196.4 0.0 copy-start.2
  196.4 0.0 reduce-scatter.3.cloned.1.call-update
  196.4 0.0 reduce-scatter.5.cloned.1.call-start
  196.5 168.9 %reduce-scatter.3.cloned.1.call-done = f32[2,8,4096]{2,1,0:T(8,128)} async-done(((f32[2,192,4096]{2,1,0:T(8,128)}), f32[2,8,4096]{2,1,0:T(8,128)}) %reduce-scatter.3.cloned.1.call-update) | async-done | bytes 262160 | tf_op jit(solution)/shard_map/reduce_scatter | solution.py:67
  365.4 0.0 reduce-scatter.5.cloned.1.call-update
  365.4 0.0 copy-done.2
  365.4 0.8 copy.25
  366.3 163.2 %reduce-scatter.5.cloned.1.call-done = f32[2,8,128]{2,1,0:T(8,128)} async-done(((f32[2,8,4096]{2,1,0:T(8,128)}), f32[2,8,128]{2,1,0:T(8,128)}) %reduce-scatter.5.cloned.1.call-update) | async-done | bytes 8208 | tf_op jit(solution)/shard_map/reduce_scatter | solution.py:68
Async XLA Ops:
  7.2 89.5 %copy-start = (bf16[1,4096,128]{2,1,0:T(8,128)(2,1)S(1)}, bf16[1,4096,128]{2,1,0:T(8,128)(2,1)}, u32[]{:S(2)}) copy-start(bf16[1,4096,128]{2,1,0:T(8,128)(2,1)} %param.9) | copy-start | bytes 3145732
  7.2 169.8 %all-gather.2.cloned.1.call-start = ((), (), s32[]{:S(2)}) async-start(), calls=%async_computation.2 | async-start | bytes 3276800 | tf_op jit(solution)/shard_map/all_gather | solution.py:59
  94.8 270.6 %reduce-scatter.3.cloned.1.call-start = ((), (), s32[]{:S(2)}) async-start(), calls=%async_computation.3 | async-start | bytes 6553600 | tf_op jit(solution)/shard_map/reduce_scatter | solution.py:67
  96.7 80.3 %copy-start.1 = (bf16[1,4096,2,128]{3,2,1,0:T(2,128)(2,1)S(1)}, bf16[1,4096,2,128]{3,2,1,0:T(2,128)(2,1)}, u32[]{:S(2)}) copy-start(bf16[1,4096,2,128]{3,2,1,0:T(2,128)(2,1)} %param.10) | copy-start | bytes 6291460
  185.7 2.0 copy-start.3
  196.4 169.0 %copy-start.2 = (bf16[2,2,64,512]{3,2,1,0:T(8,128)(2,1)S(1)}, bf16[2,2,64,512]{3,2,1,0:T(8,128)(2,1)}, u32[]{:S(2)}) copy-start(bf16[2,2,64,512]{3,2,1,0:T(8,128)(2,1)} %get-tuple-element.11) | copy-start | bytes 786436
  196.4 333.1 %reduce-scatter.5.cloned.1.call-start = ((), (), s32[]{:S(2)}) async-start(), calls=%async_computation.4 | async-start | bytes 270336 | tf_op jit(solution)/shard_map/reduce_scatter | solution.py:68
Sparse Core Ops, SparseCore 0:
  94.9 81.9 all-gather.1
  196.5 168.8 reduce-scatter.2
  369.0 160.4 reduce-scatter.4
where the time goes:
time: 537 us; the launch traced here: 536 us
  waiting for transfers between devices  405 us (75%)
  blocking collectives  87.5 us (16%)
  matrix products  20.7 us (4%)
  between operations  13.8 us (3%)
  local copies, waits for them, and re-layouts  6.14 us (1%)
    reduce_scatter x1, waiting for transfers between devices, local(): lax.psum_scatter(layer_grad, 'mp', scatter_dimension=1, tiled=True)  169 us
    reduce_scatter x1, waiting for transfers between devices, local(): lax.psum_scatter(by_heads, 'segment', scatter_dimension=2, tiled=True)  163 us
    all_gather x1, blocking collectives, local(): features = lax.all_gather(enc_out, 'segment', axis=2, tiled=True)  87.5 us
    all_gather x1, waiting for transfers between devices, local(): lax.all_gather(features, 'mp', axis=1, tiled=True)  73.1 us
  transfers between devices with their start and end apart: 3, of which 3 were waited for; matrix products, arithmetic and copies ran while one was open for 2% of the time, Pallas kernels for 0%

commit v1 on v0

--- a/solution.py
+++ b/solution.py
@@ -53,10 +53,18 @@
     query = jnp.einsum("btd,dh->bth", inputs, query_w, preferred_element_type=jnp.float32).astype(
         jnp.bfloat16
     )
-    features = lax.all_gather(enc_out, "segment", axis=2, tiled=True)
+    nb, ns, nd = enc_out.shape
+    n_mp = lax.axis_size("mp")
+    n_seg = lax.axis_size("segment")
+    gathered = lax.all_gather(enc_out, ("mp", "segment"), axis=0, tiled=False)
+    encoder = (
+        gathered.reshape(n_mp, n_seg, nb, ns, nd)
+        .transpose(2, 0, 3, 1, 4)
+        .reshape(nb, n_mp * ns, n_seg * nd)
+    )
     keyval = jnp.einsum(
         "bsd,dch->bsch",
-        lax.all_gather(features, "mp", axis=1, tiled=True),
+        encoder,
         keyval_w,
         preferred_element_type=jnp.float32,
     ).astype(jnp.bfloat16)
@@ -64,8 +72,12 @@
     usable = jnp.arange(total_src)[None, :] < src_len[:, None]
     context, dkeyval = attend_pass(query, keyval, cotangent, usable)
     layer_grad = jnp.einsum("bsch,dch->bsd", dkeyval, keyval_w, preferred_element_type=jnp.float32)
-    by_heads = lax.psum_scatter(layer_grad, "mp", scatter_dimension=1, tiled=True)
-    d_enc = lax.psum_scatter(by_heads, "segment", scatter_dimension=2, tiled=True)
+    blocks = (
+        layer_grad.reshape(nb, n_mp, ns, n_seg, nd)
+        .transpose(1, 3, 0, 2, 4)
+        .reshape(n_mp * n_seg, nb, ns, nd)
+    )
+    d_enc = lax.psum_scatter(blocks, ("mp", "segment"), scatter_dimension=0, tiled=False)
     return (context[:, None], d_enc)
 
 

time: 537 us -> 5420 us (10.09)
  the two profiles are of different devices: /device:TPU:6 before, /device:TPU:512 now
where the time goes in v1:
time: 5420 us
  waiting for transfers between devices  5370 us (99%)
    reduce_scatter x1, waiting for transfers between devices, local(): lax.psum_scatter(blocks, ('mp', 'segment'), scatter_dimension=0, tiled=Fa...  3800 us
    all_gather x1, waiting for transfers between devices, local(): gathered = lax.all_gather(enc_out, ('mp', 'segment'), axis=0, tiled=False)  1570 us
  transfers between devices with their start and end apart: 2, of which 2 were waited for; matrix products, arithmetic and copies ran while one was open for 0% of the time, Pallas kernels for 0%

profile of v1, /device:TPU:512, one launch (start us, length us, event | category | flops | bytes accessed | tf_op | source)
XLA Modules:
  0.0 5420.6 jit_solution(8205475836215109605)
XLA Ops:
  7.2 0.0 copy-start
  7.2 0.0 all-gather.3.cloned.1.call-start
  7.2 0.7 all-gather.3.cloned.1.call-update
  7.9 0.0 reduce-scatter.2.cloned.1.call-start
  8.0 1.1 copy.37
  9.1 0.7 iota_compare_fusion
  9.8 0.0 copy-done
  9.8 0.0 copy-start.1
  9.8 7.1 fusion.15
  16.9 1570.4 %all-gather.3.cloned.1.call-done = bf16[1536,8,128]{2,1,0:T(8,128)(2,1)} async-done(((bf16[2,8,128]{2,1,0:T(8,128)(2,1)}), bf16[1536,8,128]{2,1,0:T(8,128)(2,1)}) %all-gather.3.cloned.1.call-update) | async-done | bytes 3145744 | tf_op jit(solution)/shard_map/all_gather | solution.py:59
  1587.3 0.0 copy-done.1
  1587.3 2.9 fusion.18
  1590.2 0.6 fusion.38
  1590.8 1.7 copy.36
  1592.5 0.8 copy.34
  1593.2 2.8 fusion.39
  1596.0 0.0 copy-start.3
  1596.0 1.6 fusion.29
  1597.7 0.4 fusion.24
  1598.1 0.0 copy-done.3
  1598.1 1.0 fusion.30
  1599.1 2.9 fusion.25
  1601.9 1.1 copy.38
  1603.0 0.8 stack.7
  1603.8 0.2 copy.39
  1603.9 0.1 stack.8
  1604.1 1.9 fusion.6
  1606.0 3.2 copy.43
  1609.1 0.0 copy-start.2
  1609.1 0.0 reduce-scatter.2.cloned.1.call-update
  1609.2 0.9 copy-done.2
  1610.1 0.8 copy.44
  1610.9 3802.9 %reduce-scatter.2.cloned.1.call-done = f32[1,2,8,128]{3,2,1,0:T(8,128)} async-done(((f32[768,2,8,128]{3,2,1,0:T(8,128)}), f32[1,2,8,128]{3,2,1,0:T(8,128)}) %reduce-scatter.2.cloned.1.call-update) | async-done | bytes 8208 | tf_op jit(solution)/shard_map/reduce_scatter | solution.py:80
Async XLA Ops:
  7.2 2.6 copy-start
  7.2 1580.1 %all-gather.3.cloned.1.call-start = ((), (), s32[]{:S(2)}) async-start(), calls=%async_computation.2 | async-start | bytes 3149824 | tf_op jit(solution)/shard_map/all_gather | solution.py:59
  7.9 5405.9 %reduce-scatter.2.cloned.1.call-start = ((), (), s32[]{:S(2)}) async-start(), calls=%async_computation.1 | async-start | bytes 6299648 | tf_op jit(solution)/shard_map/reduce_scatter | solution.py:80
  9.8 1577.5 %copy-start.1 = (bf16[1,4096,2,128]{3,2,1,0:T(2,128)(2,1)S(1)}, bf16[1,4096,2,128]{3,2,1,0:T(2,128)(2,1)}, u32[]{:S(2)}) copy-start(bf16[1,4096,2,128]{3,2,1,0:T(2,128)(2,1)} %param.10) | copy-start | bytes 6291460
  1596.0 2.0 copy-start.3
  1609.1 0.9 copy-start.2
Sparse Core Ops, SparseCore 0:
  10.5 1576.7 all-gather.2
  1609.3 3804.4 reduce-scatter.1

commit v2 on v0

--- a/solution.py
+++ b/solution.py
@@ -4,6 +4,9 @@
 import jax.numpy as jnp
 from jax import lax
 from jax.sharding import PartitionSpec as P
+from jax.experimental import pallas as pl
+from jax.experimental.pallas import tpu as pltpu
+import functools
 
 HD = 64
 
@@ -45,6 +48,65 @@
     return (context.reshape(num_batch, num_tgt, width), dkeyval)
 
 
+def _exchange_kernel(axis, n, gather, x_ref, y_ref, send_sem, recv_sem, local_sem):
+    me = lax.axis_index(axis)
+    mesh_ids = pl.DeviceIdType.MESH
+    barrier = pltpu.get_barrier_semaphore()
+
+    def greet(k, carry):
+        peer = lax.rem(me + k, n)
+        pl.semaphore_signal(barrier, inc=1, device_id={axis: peer}, device_id_type=mesh_ids)
+        return carry
+
+    lax.fori_loop(1, n, greet, 0)
+    pl.semaphore_wait(barrier, n - 1)
+
+    def send(k, carry):
+        peer = lax.rem(me + k, n)
+        block = x_ref if gather else x_ref.at[peer]
+        pltpu.make_async_remote_copy(
+            src_ref=block,
+            dst_ref=y_ref.at[me],
+            send_sem=send_sem,
+            recv_sem=recv_sem,
+            device_id={axis: peer},
+            device_id_type=mesh_ids,
+        ).start()
+        return carry
+
+    lax.fori_loop(1, n, send, 0)
+    own = pltpu.make_async_copy(x_ref if gather else x_ref.at[me], y_ref.at[me], local_sem)
+    own.start()
+    own.wait()
+    every = pltpu.make_async_remote_copy(
+        src_ref=y_ref.at[pl.ds(0, n - 1)],
+        dst_ref=y_ref.at[pl.ds(0, n - 1)],
+        send_sem=send_sem,
+        recv_sem=recv_sem,
+        device_id={axis: lax.rem(me + 1, n)},
+        device_id_type=mesh_ids,
+    )
+    every.wait_send()
+    every.wait_recv()
+
+
+def exchange(x, axis, n, cid, gather):
+    block = x.shape if gather else x.shape[1:]
+    out_shape = jax.ShapeDtypeStruct((n,) + tuple(block), x.dtype)
+    return pl.pallas_call(
+        functools.partial(_exchange_kernel, axis, n, gather),
+        out_shape=out_shape,
+        in_specs=[pl.BlockSpec(memory_space=pl.ANY)],
+        out_specs=pl.BlockSpec(memory_space=pl.ANY),
+        scratch_shapes=[
+            pltpu.SemaphoreType.DMA,
+            pltpu.SemaphoreType.DMA,
+            pltpu.SemaphoreType.DMA,
+        ],
+        compiler_params=pltpu.CompilerParams(collective_id=cid, has_side_effects=True),
+    )(x)
+
+
 def local(enc_out, dec_in, grad_context, w_query, w_keyval, src_len):
     inputs = dec_in[:, 0]
     cotangent = grad_context[:, 0]
@@ -53,19 +115,29 @@
     query = jnp.einsum("btd,dh->bth", inputs, query_w, preferred_element_type=jnp.float32).astype(
         jnp.bfloat16
     )
-    features = lax.all_gather(enc_out, "segment", axis=2, tiled=True)
+    nb, ns, nd = enc_out.shape
+    n_mp = lax.axis_size("mp")
+    n_seg = lax.axis_size("segment")
+    by_feature = exchange(enc_out, "segment", n_seg, 0, True)
+    features = by_feature.transpose(1, 2, 0, 3).reshape(nb, ns, n_seg * nd)
+    by_source = exchange(features, "mp", n_mp, 1, True)
+    encoder = by_source.transpose(1, 0, 2, 3).reshape(nb, n_mp * ns, n_seg * nd)
     keyval = jnp.einsum(
         "bsd,dch->bsch",
-        lax.all_gather(features, "mp", axis=1, tiled=True),
+        encoder,
         keyval_w,
         preferred_element_type=jnp.float32,
     ).astype(jnp.bfloat16)
     total_src = keyval.shape[1]
     usable = jnp.arange(total_src)[None, :] < src_len[:, None]
     context, dkeyval = attend_pass(query, keyval, cotangent, usable)
-    layer_grad = jnp.einsum("bsch,dch->bsd", dkeyval, keyval_w, preferred_element_type=jnp.float32)
-    by_heads = lax.psum_scatter(layer_grad, "mp", scatter_dimension=1, tiled=True)
-    d_enc = lax.psum_scatter(by_heads, "segment", scatter_dimension=2, tiled=True)
+    grad_blocks = dkeyval.reshape(nb, n_mp, ns, *dkeyval.shape[2:])
+    layer_grad = jnp.einsum(
+        "bmsch,dch->mbsd", grad_blocks, keyval_w, preferred_element_type=jnp.float32
+    )
+    by_heads = exchange(layer_grad, "mp", n_mp, 2, False).sum(axis=0)
+    split = by_heads.reshape(nb, ns, n_seg, nd).transpose(2, 0, 1, 3)
+    d_enc = exchange(split, "segment", n_seg, 3, False).sum(axis=0)
     return (context[:, None], d_enc)
 
 

time: 537 us -> 437 us (0.81)
  Pallas kernels: 0 us -> 407 us
  waiting for transfers between devices: 405 us -> 0 us
  blocking collectives: 87.5 us -> 0 us
  between operations: 13.8 us -> 0.79 us
    pallas_call x0 -> x4, Pallas kernels: none -> 407 us  [exchange(): pl.pallas_call(functools.partial(_exchange_kernel, axis, n, gather), out_...]
    reduce_scatter x2 -> x0, waiting for transfers between devices: 332 us -> none  [the longest x1 169 us: local(): lax.psum_scatter(layer_grad, 'mp', scatter_dimension=1, tiled=True)]
    all_gather x1 -> x0, blocking collectives: 87.5 us -> none  [local(): features = lax.all_gather(enc_out, 'segment', axis=2, tiled=True)]
    all_gather x1 -> x0, waiting for transfers between devices: 73.1 us -> none  [local(): lax.all_gather(features, 'mp', axis=1, tiled=True)]
  transfers between devices with their start and end apart: 3 -> 0, of which waited for: 3 -> 0; matrix products, arithmetic and copies ran while one was open for 2% -> 0% of each run, Pallas kernels for 0% -> 0%
where the time goes in v2:
time: 437 us
  Pallas kernels  407 us (93%)
  matrix products  18 us (4%)
  other arithmetic  5.7 us (1%)
  local copies, waits for them, and re-layouts  5.03 us (1%)
    pallas_call x4, Pallas kernels, exchange(): pl.pallas_call(functools.partial(_exchange_kernel, axis, n, gather), out_...  407 us

profile of v2, /device:TPU:6, one launch (start us, length us, event | category | flops | bytes accessed | tf_op | source)
XLA Modules:
  0.0 436.7 jit_solution(4463636943895243689)
XLA Ops:
  0.6 0.0 copy-start
  0.6 0.8 iota_compare_fusion
  1.5 16.8 %shard_map.77 = bf16[32,2,8,128]{3,2,1,0:T(8,128)(2,1)} custom-call(bf16[2,8,128]{2,1,0:T(8,128)(2,1)} %x_ref.1), custom_call_target="tpu_custom_call" | custom-call | tf_op jit(solution)/shard_map/pallas_call | solution.py:96
  18.3 1.6 copy_bitcast_fusion.x_ref
  19.9 1.1 copy.25
  20.9 0.0 copy-done
  21.0 6.3 %fusion.15 = bf16[2,512,128]{1,2,0:T(8,128)(2,1)S(1)} fusion(bf16[2,1,512,4096]{3,2,1,0:T(8,128)(2,1)} %param.7, bf16[1,4096,128]{2,1,0:T(8,128)(2,1)S(1)} %copy-done), kind=kOutput, calls=%fused_computation.18 | convolution fusion | flops 1073872896 | bytes 9699328 | tf_op jit(solution)/shard_map/btd,dh->bth/dot_general | solution.py:115
  27.2 0.0 copy-start.1
  27.3 118.3 %shard_map.78 = bf16[24,2,8,4096]{3,2,1,0:T(8,128)(2,1)} custom-call(bf16[2,8,4096]{2,1,0:T(8,128)(2,1)} %copy_bitcast_fusion.x_ref), custom_call_target="tpu_custom_call" | custom-call | tf_op jit(solution)/shard_map/pallas_call | solution.py:96
  145.5 3.5 fusion.18
  149.1 0.1 copy.24
  149.2 0.1 copy.22
  149.3 0.0 copy-done.1
  149.3 0.7 fusion.37
  150.0 0.2 fusion.29
  150.2 0.4 fusion.24
  150.6 0.3 fusion.30
  150.9 1.6 fusion.25
  152.5 0.8 copy.33
  153.3 0.2 copy.26
  153.5 0.1 stack.7
  153.6 0.2 copy.27
  153.8 0.1 stack.8
  153.9 5.3 %convolution_bitcast_fusion.x_ref = f32[24,2,8,4096]{3,2,1,0:T(8,128)} fusion(bf16[4096,2,128]{2,1,0:T(2,128)(2,1)} %bitcast.100, bf16[2,24,8,1,128]{4,2,3,1,0:T(8,128)(2,1)S(1)} %bitcast.98, bf16[2,24,8,1,128]{4,2,3,1,0:T(8,128)(2,1)S(1)} %bitcast.97), kind=kOutput, calls=%fused_computation.3 | convolution fusion | flops 805404672 | bytes 8585216 | tf_op jit(solution)/shard_map/bmsch,dch->mbsd/dot_general | solution.py:135
  159.2 201.3 %shard_map.79 = f32[24,2,8,4096]{3,2,1,0:T(8,128)} custom-call(f32[24,2,8,4096]{3,2,1,0:T(8,128)} %convolution_bitcast_fusion.x_ref), custom_call_target="tpu_custom_call" | custom-call | tf_op jit(solution)/shard_map/pallas_call | solution.py:96
  360.5 3.1 reduce_sum.28
  363.6 0.7 bitcast_bitcast_fusion.x_ref
  364.3 70.8 %shard_map.80 = f32[32,2,8,128]{3,2,1,0:T(8,128)} custom-call(f32[32,2,8,128]{3,2,1,0:T(8,128)} %bitcast_bitcast_fusion.x_ref), custom_call_target="tpu_custom_call" | custom-call | tf_op jit(solution)/shard_map/pallas_call | solution.py:96
  435.1 1.6 reduce_sum.29
  (1 shorter events, 0.0 us)
Async XLA Ops:
  0.6 20.3 %copy-start = (bf16[1,4096,128]{2,1,0:T(8,128)(2,1)S(1)}, bf16[1,4096,128]{2,1,0:T(8,128)(2,1)}, u32[]{:S(2)}) copy-start(bf16[1,4096,128]{2,1,0:T(8,128)(2,1)} %param.9) | copy-start | bytes 3145732
  27.2 122.1 %copy-start.1 = (bf16[2,512,128]{1,2,0:T(8,128)(2,1)}, bf16[2,512,128]{1,2,0:T(8,128)(2,1)S(1)}, u32[]{:S(2)}) copy-start(bf16[2,512,128]{1,2,0:T(8,128)(2,1)S(1)} %fusion.15) | copy-start | bytes 786436

commit v3 on v2

--- a/solution.py
+++ b/solution.py
@@ -48,53 +48,57 @@
     return (context.reshape(num_batch, num_tgt, width), dkeyval)
 
 
-def _exchange_kernel(axis, n, gather, x_ref, y_ref, send_sem, recv_sem, local_sem):
+def _exchange_kernel(axis, stride, count, gather, x_ref, y_ref, send_sem, recv_sem, local_sem):
     me = lax.axis_index(axis)
+    digit = lax.rem(lax.div(me, stride), count)
+    base = me - digit * stride
     mesh_ids = pl.DeviceIdType.MESH
     barrier = pltpu.get_barrier_semaphore()
 
+    def peer_of(k):
+        return base + lax.rem(digit + k, count) * stride
+
     def greet(k, carry):
-        peer = lax.rem(me + k, n)
-        pl.semaphore_signal(barrier, inc=1, device_id={axis: peer}, device_id_type=mesh_ids)
+        pl.semaphore_signal(barrier, inc=1, device_id={axis: peer_of(k)}, device_id_type=mesh_ids)
         return carry
 
-    lax.fori_loop(1, n, greet, 0)
-    pl.semaphore_wait(barrier, n - 1)
+    lax.fori_loop(1, count, greet, 0)
+    pl.semaphore_wait(barrier, count - 1)
 
     def send(k, carry):
-        peer = lax.rem(me + k, n)
-        block = x_ref if gather else x_ref.at[peer]
+        slot = lax.rem(digit + k, count)
+        block = x_ref if gather else x_ref.at[slot]
         pltpu.make_async_remote_copy(
             src_ref=block,
-            dst_ref=y_ref.at[me],
+            dst_ref=y_ref.at[digit],
             send_sem=send_sem,
             recv_sem=recv_sem,
-            device_id={axis: peer},
+            device_id={axis: base + slot * stride},
             device_id_type=mesh_ids,
         ).start()
         return carry
 
-    lax.fori_loop(1, n, send, 0)
-    own = pltpu.make_async_copy(x_ref if gather else x_ref.at[me], y_ref.at[me], local_sem)
+    lax.fori_loop(1, count, send, 0)
+    own = pltpu.make_async_copy(x_ref if gather else x_ref.at[digit], y_ref.at[digit], local_sem)
     own.start()
     own.wait()
     every = pltpu.make_async_remote_copy(
-        src_ref=y_ref.at[pl.ds(0, n - 1)],
-        dst_ref=y_ref.at[pl.ds(0, n - 1)],
+        src_ref=y_ref.at[pl.ds(0, count - 1)],
+        dst_ref=y_ref.at[pl.ds(0, count - 1)],
         send_sem=send_sem,
         recv_sem=recv_sem,
-        device_id={axis: lax.rem(me + 1, n)},
+        device_id={axis: peer_of(1)},
         device_id_type=mesh_ids,
     )
     every.wait_send()
     every.wait_recv()
 
 
-def exchange(x, axis, n, cid, gather):
+def exchange(x, axis, stride, count, cid, gather):
     block = x.shape if gather else x.shape[1:]
-    out_shape = jax.ShapeDtypeStruct((n,) + tuple(block), x.dtype)
+    out_shape = jax.ShapeDtypeStruct((count,) + tuple(block), x.dtype)
     return pl.pallas_call(
-        functools.partial(_exchange_kernel, axis, n, gather),
+        functools.partial(_exchange_kernel, axis, stride, count, gather),
         out_shape=out_shape,
         in_specs=[pl.BlockSpec(memory_space=pl.ANY)],
         out_specs=pl.BlockSpec(memory_space=pl.ANY),
@@ -118,10 +122,15 @@
     nb, ns, nd = enc_out.shape
     n_mp = lax.axis_size("mp")
     n_seg = lax.axis_size("segment")
-    by_feature = exchange(enc_out, "segment", n_seg, 0, True)
+    n_core = 2
+    n_x = n_mp // (n_core * 3)
+    n_z = n_mp // (n_core * n_x)
+    by_feature = exchange(enc_out, "segment", 1, n_seg, 0, True)
     features = by_feature.transpose(1, 2, 0, 3).reshape(nb, ns, n_seg * nd)
-    by_source = exchange(features, "mp", n_mp, 1, True)
-    encoder = by_source.transpose(1, 0, 2, 3).reshape(nb, n_mp * ns, n_seg * nd)
+    by_z = exchange(features, "mp", n_x * n_core, n_z, 1, True)
+    by_x = exchange(by_z, "mp", n_core, n_x, 2, True)
+    by_core = exchange(by_x, "mp", 1, n_core, 3, True)
+    encoder = by_core.transpose(3, 2, 1, 0, 4, 5).reshape(nb, n_mp * ns, n_seg * nd)
     keyval = jnp.einsum(
         "bsd,dch->bsch",
         encoder,
@@ -131,13 +140,15 @@
     total_src = keyval.shape[1]
     usable = jnp.arange(total_src)[None, :] < src_len[:, None]
     context, dkeyval = attend_pass(query, keyval, cotangent, usable)
-    grad_blocks = dkeyval.reshape(nb, n_mp, ns, *dkeyval.shape[2:])
+    grad_blocks = dkeyval.reshape(nb, n_z, n_x, n_core, ns, *dkeyval.shape[2:])
     layer_grad = jnp.einsum(
-        "bmsch,dch->mbsd", grad_blocks, keyval_w, preferred_element_type=jnp.float32
+        "bzxwsch,dch->wxzbsd", grad_blocks, keyval_w, preferred_element_type=jnp.float32
     )
-    by_heads = exchange(layer_grad, "mp", n_mp, 2, False).sum(axis=0)
+    over_core = exchange(layer_grad, "mp", 1, n_core, 4, False).sum(axis=0)
+    over_x = exchange(over_core, "mp", n_core, n_x, 5, False).sum(axis=0)
+    by_heads = exchange(over_x, "mp", n_x * n_core, n_z, 6, False).sum(axis=0)
     split = by_heads.reshape(nb, ns, n_seg, nd).transpose(2, 0, 1, 3)
-    d_enc = exchange(split, "segment", n_seg, 3, False).sum(axis=0)
+    d_enc = exchange(split, "segment", 1, n_seg, 7, False).sum(axis=0)
     return (context[:, None], d_enc)
 
 

time: 437 us -> 327 us (0.75)
  Pallas kernels: 407 us -> 290 us
  other arithmetic: 5.7 us -> 12.1 us
    pallas_call x4 -> x8, Pallas kernels: 407 us -> 290 us  [exchange(): pl.pallas_call(functools.partial(_exchange_kernel, axis, stride, count, g...]
    reduce_sum x2 -> x4, other arithmetic: 4.68 us -> 11.1 us  [the longest x1 5.24 us: local(): over_core = exchange(layer_grad, 'mp', 1, n_core, 4, False).sum(axis=0)]
where the time goes in v3:
time: 327 us; the launch traced here: 326 us
  Pallas kernels  290 us (89%)
  matrix products  15.5 us (5%)
  other arithmetic  12.1 us (4%)
  local copies, waits for them, and re-layouts  7.56 us (2%)
    pallas_call x8, Pallas kernels, exchange(): pl.pallas_call(functools.partial(_exchange_kernel, axis, stride, count, g...  290 us

profile of v3, /device:TPU:6, one launch (start us, length us, event | category | flops | bytes accessed | tf_op | source)
XLA Modules:
  0.0 326.1 jit_solution(8764186509923135667)
XLA Ops:
  0.6 0.0 copy-start
  0.6 0.8 iota_compare_fusion
  1.5 16.8 %shard_map.77 = bf16[32,2,8,128]{3,2,1,0:T(8,128)(2,1)} custom-call(bf16[2,8,128]{2,1,0:T(8,128)(2,1)} %x_ref.1), custom_call_target="tpu_custom_call" | custom-call | tf_op jit(solution)/shard_map/pallas_call | solution.py:100
  18.3 1.6 copy_bitcast_fusion.x_ref
  19.9 1.1 copy.25
  21.0 24.0 %shard_map.78.x_ref = bf16[3,2,8,4096]{3,2,1,0:T(8,128)(2,1)} custom-call(bf16[2,8,4096]{2,1,0:T(8,128)(2,1)} %copy_bitcast_fusion.x_ref), custom_call_target="tpu_custom_call" | custom-call | tf_op jit(solution)/shard_map/pallas_call | solution.py:100
  45.0 0.0 copy-done
  45.0 6.3 %fusion.13 = bf16[2,512,128]{1,2,0:T(8,128)(2,1)S(1)} fusion(bf16[2,1,512,4096]{3,2,1,0:T(8,128)(2,1)} %param.7, bf16[1,4096,128]{2,1,0:T(8,128)(2,1)S(1)} %copy-done), kind=kOutput, calls=%fused_computation.16 | convolution fusion | flops 1073872896 | bytes 9699328 | tf_op jit(solution)/shard_map/btd,dh->bth/dot_general | solution.py:119
  51.3 0.0 copy-start.1
  51.3 21.6 %shard_map.79.x_ref = bf16[4,3,2,8,4096]{4,3,2,1,0:T(8,128)(2,1)} custom-call(bf16[3,2,8,4096]{3,2,1,0:T(8,128)(2,1)} %shard_map.78.x_ref), custom_call_target="tpu_custom_call" | custom-call | tf_op jit(solution)/shard_map/pallas_call | solution.py:100
  72.9 49.5 %shard_map.80 = bf16[2,4,3,2,8,4096]{5,4,3,2,1,0:T(8,128)(2,1)} custom-call(bf16[4,3,2,8,4096]{4,3,2,1,0:T(8,128)(2,1)} %shard_map.79.x_ref), custom_call_target="tpu_custom_call" | custom-call | tf_op jit(solution)/shard_map/pallas_call | solution.py:100
  122.4 0.0 copy-start.2
  122.5 2.4 copy.20
  124.8 0.1 copy-done.2
  125.0 1.0 fusion.16
  126.0 0.1 copy.24
  126.1 0.1 copy.22
  126.2 0.0 copy-done.1
  126.2 0.7 fusion.33
  126.9 0.2 fusion.25
  127.2 0.4 fusion.20
  127.5 0.3 fusion.26
  127.8 1.6 fusion.21
  129.4 0.8 copy.33
  130.2 0.2 copy.26
  130.4 0.1 stack.7
  130.5 0.2 copy.27
  130.7 0.1 stack.8
  130.8 5.3 %convolution_bitcast_fusion.x_ref = f32[2,4,3,2,8,4096]{5,4,3,2,1,0:T(8,128)} fusion(bf16[4096,2,128]{2,1,0:T(2,128)(2,1)} %bitcast.95, bf16[2,3,4,2,8,1,128]{6,4,5,3,2,1,0:T(8,128)(2,1)S(1)} %bitcast.94, bf16[2,3,4,2,8,1,128]{6,4,5,3,2,1,0:T(8,128)(2,1)S(1)} %bitcast.93), kind=kOutput, calls=%fused_computation.3 | convolution fusion | flops 805404672 | bytes 8585216 | tf_op jit(solution)/shard_map/bzxwsch,dch->wxzbsd/dot_general | solution.py:144
  136.1 97.6 %shard_map.81 = f32[2,4,3,2,8,4096]{5,4,3,2,1,0:T(8,128)} custom-call(f32[2,4,3,2,8,4096]{5,4,3,2,1,0:T(8,128)} %convolution_bitcast_fusion.x_ref), custom_call_target="tpu_custom_call" | custom-call | tf_op jit(solution)/shard_map/pallas_call | solution.py:100
  233.8 5.2 %reduce_sum.46.x_ref = f32[4,3,2,8,4096]{4,3,2,1,0:T(8,128)} reduce(f32[2,4,3,2,8,4096]{5,4,3,2,1,0:T(8,128)} %shard_map.81, f32[]{:T(128)} %constant.3.clone.1), dimensions={0}, to_apply=%region_2.3 | reduce | flops 786432 | bytes 9437188 | tf_op jit(solution)/shard_map/reduce_sum | solution.py:147
  239.0 38.8 %shard_map.82 = f32[4,3,2,8,4096]{4,3,2,1,0:T(8,128)} custom-call(f32[4,3,2,8,4096]{4,3,2,1,0:T(8,128)} %reduce_sum.46.x_ref), custom_call_target="tpu_custom_call" | custom-call | tf_op jit(solution)/shard_map/pallas_call | solution.py:100
  277.9 3.0 reduce_sum.47.x_ref
  280.9 29.1 %shard_map.83 = f32[3,2,8,4096]{3,2,1,0:T(8,128)} custom-call(f32[3,2,8,4096]{3,2,1,0:T(8,128)} %reduce_sum.47.x_ref), custom_call_target="tpu_custom_call" | custom-call | tf_op jit(solution)/shard_map/pallas_call | solution.py:100
  310.0 1.2 reduce_sum.48
  311.2 0.7 bitcast_bitcast_fusion.x_ref
  311.9 12.6 %shard_map.84 = f32[32,2,8,128]{3,2,1,0:T(8,128)} custom-call(f32[32,2,8,128]{3,2,1,0:T(8,128)} %bitcast_bitcast_fusion.x_ref), custom_call_target="tpu_custom_call" | custom-call | tf_op jit(solution)/shard_map/pallas_call | solution.py:100
  324.5 1.6 reduce_sum.49
  (1 shorter events, 0.0 us)
Async XLA Ops:
  0.6 44.3 %copy-start = (bf16[1,4096,128]{2,1,0:T(8,128)(2,1)S(1)}, bf16[1,4096,128]{2,1,0:T(8,128)(2,1)}, u32[]{:S(2)}) copy-start(bf16[1,4096,128]{2,1,0:T(8,128)(2,1)} %param.9) | copy-start | bytes 3145732
  51.3 75.0 %copy-start.1 = (bf16[2,512,128]{1,2,0:T(8,128)(2,1)}, bf16[2,512,128]{1,2,0:T(8,128)(2,1)S(1)}, u32[]{:S(2)}) copy-start(bf16[2,512,128]{1,2,0:T(8,128)(2,1)S(1)} %fusion.13) | copy-start | bytes 786436
  122.4 2.5 copy-start.2

commit v4 on v3

--- a/solution.py
+++ b/solution.py
@@ -48,29 +48,30 @@
     return (context.reshape(num_batch, num_tgt, width), dkeyval)
 
 
-def _exchange_kernel(axis, stride, count, gather, x_ref, y_ref, send_sem, recv_sem, local_sem):
+def _exchange_kernel(axis, stride, count, gather, x_ref, y_ref, send_sem, recv_sem):
     me = lax.axis_index(axis)
     digit = lax.rem(lax.div(me, stride), count)
     base = me - digit * stride
+    pieces = y_ref.shape[1]
     mesh_ids = pl.DeviceIdType.MESH
     barrier = pltpu.get_barrier_semaphore()
 
-    def peer_of(k):
-        return base + lax.rem(digit + k, count) * stride
-
     def greet(k, carry):
-        pl.semaphore_signal(barrier, inc=1, device_id={axis: peer_of(k)}, device_id_type=mesh_ids)
+        peer = base + lax.rem(digit + k, count) * stride
+        pl.semaphore_signal(barrier, inc=1, device_id={axis: peer}, device_id_type=mesh_ids)
         return carry
 
     lax.fori_loop(1, count, greet, 0)
     pl.semaphore_wait(barrier, count - 1)
 
-    def send(k, carry):
+    def send(i, carry):
+        k = 1 + lax.div(i, pieces)
+        p = lax.rem(i, pieces)
         slot = lax.rem(digit + k, count)
-        block = x_ref if gather else x_ref.at[slot]
+        block = x_ref.at[p] if gather else x_ref.at[slot, p]
         pltpu.make_async_remote_copy(
             src_ref=block,
-            dst_ref=y_ref.at[digit],
+            dst_ref=y_ref.at[digit, p],
             send_sem=send_sem,
             recv_sem=recv_sem,
             device_id={axis: base + slot * stride},
@@ -78,16 +79,13 @@
         ).start()
         return carry
 
-    lax.fori_loop(1, count, send, 0)
-    own = pltpu.make_async_copy(x_ref if gather else x_ref.at[digit], y_ref.at[digit], local_sem)
-    own.start()
-    own.wait()
+    lax.fori_loop(0, (count - 1) * pieces, send, 0)
     every = pltpu.make_async_remote_copy(
         src_ref=y_ref.at[pl.ds(0, count - 1)],
         dst_ref=y_ref.at[pl.ds(0, count - 1)],
         send_sem=send_sem,
         recv_sem=recv_sem,
-        device_id={axis: peer_of(1)},
+        device_id={axis: base + lax.rem(digit + 1, count) * stride},
         device_id_type=mesh_ids,
     )
     every.wait_send()
@@ -96,19 +94,22 @@
 
 def exchange(x, axis, stride, count, cid, gather):
     block = x.shape if gather else x.shape[1:]
-    out_shape = jax.ShapeDtypeStruct((count,) + tuple(block), x.dtype)
-    return pl.pallas_call(
+    lead = () if gather else (count,)
+    pieces = math.prod(block[:-2])
+    parts = x.reshape(lead + (pieces, -1) + tuple(block[-2:]))
+    out_shape = jax.ShapeDtypeStruct((count,) + parts.shape[len(lead):], x.dtype)
+    received = pl.pallas_call(
         functools.partial(_exchange_kernel, axis, stride, count, gather),
         out_shape=out_shape,
         in_specs=[pl.BlockSpec(memory_space=pl.ANY)],
         out_specs=pl.BlockSpec(memory_space=pl.ANY),
-        scratch_shapes=[
-            pltpu.SemaphoreType.DMA,
-            pltpu.SemaphoreType.DMA,
-            pltpu.SemaphoreType.DMA,
-        ],
+        scratch_shapes=[pltpu.SemaphoreType.DMA, pltpu.SemaphoreType.DMA],
         compiler_params=pltpu.CompilerParams(collective_id=cid, has_side_effects=True),
-    )(x)
+    )(parts).reshape((count,) + tuple(block))
+    digit = lax.rem(lax.div(lax.axis_index(axis), stride), count)
+    mine = (jnp.arange(count) == digit).reshape((count,) + (1,) * len(block))
+    own = x[None] if gather else x
+    return jnp.where(mine, own, received)
 
 
 def local(enc_out, dec_in, grad_context, w_query, w_keyval, src_len):

time: 327 us -> 204 us (0.62)
  Pallas kernels: 290 us -> 155 us
  other arithmetic: 12.1 us -> 22.1 us
  local copies, waits for them, and re-layouts: 7.56 us -> 11.5 us
    pallas_call x8, Pallas kernels: 290 us -> 155 us  [exchange(): pl.pallas_call(functools.partial(_exchange_kernel, axis, stride, count, g...]
    select_n x0 -> x4, other arithmetic: none -> 6.45 us  [exchange(): return jnp.where(mine, own, received)]
where the time goes in v4:
time: 204 us; the launch traced here: 203 us
  Pallas kernels  155 us (76%)
  other arithmetic  22.1 us (11%)
  matrix products  13.5 us (7%)
  local copies, waits for them, and re-layouts  11.5 us (6%)
    pallas_call x8, Pallas kernels, exchange(): pl.pallas_call(functools.partial(_exchange_kernel, axis, stride, count, g...  155 us
    dot_general x1, matrix products, local(): jnp.einsum('btd,dh->bth', inputs, query_w, preferred_element_type=jnp.flo...  7.04 us
    select_n x4, other arithmetic, exchange(): return jnp.where(mine, own, received)  6.45 us
    reduce_sum x1, other arithmetic, local(): over_core = exchange(layer_grad, 'mp', 1, n_core, 4, False).sum(axis=0)  6.28 us
    reduce_sum x1, other arithmetic, local(): over_x = exchange(over_core, 'mp', n_core, n_x, 5, False).sum(axis=0)  4.41 us

profile of v4, /device:TPU:6, one launch (start us, length us, event | category | flops | bytes accessed | tf_op | source)
XLA Modules:
  0.0 203.2 jit_solution(13841681973414472939)
XLA Ops:
  0.6 0.0 copy-start
  0.6 0.0 copy-start.6
  0.7 0.0 copy-start.7
  0.7 0.0 copy-start.13
  0.8 0.0 copy-start.9
  0.8 0.0 copy-start.11
  0.8 0.1 broadcast_in_dim.137
  0.9 0.1 broadcast_in_dim.138
  1.0 0.7 iota_compare_fusion
  1.7 0.1 broadcast_in_dim.142
  1.8 0.1 broadcast_in_dim.143
  1.8 16.8 %shard_map.77 = bf16[32,2,1,8,128]{4,3,2,1,0:T(8,128)(2,1)} custom-call(bf16[2,1,8,128]{3,2,1,0:T(8,128)(2,1)} %bitcast.163), custom_call_target="tpu_custom_call" | custom-call | tf_op jit(solution)/shard_map/pallas_call | solution.py:101
  18.7 1.0 fusion.33
  19.7 0.0 copy-done.11
  19.8 0.7 reshape_reshape.3
  20.5 24.0 %shard_map.78 = bf16[3,2,1,8,4096]{4,3,2,1,0:T(8,128)(2,1)} custom-call(bf16[2,1,8,4096]{3,2,1,0:T(8,128)(2,1)} %bitcast.155), custom_call_target="tpu_custom_call" | custom-call | tf_op jit(solution)/shard_map/pallas_call | solution.py:101
  44.5 0.0 copy-done.6
  44.5 0.1 copy.52
  44.6 0.0 copy-done
  44.7 0.0 copy-start.4
  44.7 7.0 %fusion.13 = bf16[2,512,128]{1,2,0:T(8,128)(2,1)} fusion(bf16[2,1,512,4096]{3,2,1,0:T(8,128)(2,1)} %param.7, bf16[1,4096,128]{2,1,0:T(8,128)(2,1)S(1)} %copy-done), kind=kOutput, calls=%fused_computation.21 | convolution fusion | flops 1073872896 | bytes 9699328 | tf_op jit(solution)/shard_map/btd,dh->bth/dot_general | solution.py:120
  51.7 0.0 copy-done.13
  51.7 0.0 copy-done.4
  51.7 0.1 bitcast_select_fusion.4
  51.8 0.8 bitcast_select_fusion.3.x_ref
  52.7 21.6 %shard_map.79 = bf16[4,6,1,8,4096]{4,3,2,1,0:T(8,128)(2,1)} custom-call(bf16[6,1,8,4096]{3,2,1,0:T(8,128)(2,1)} %bitcast_select_fusion.3.x_ref), custom_call_target="tpu_custom_call" | custom-call | tf_op jit(solution)/shard_map/pallas_call | solution.py:101
  74.3 0.0 copy-start.2
  74.3 0.2 broadcast_in_dim.136
  74.5 1.2 copy-done.2
  75.7 1.4 bitcast_select_fusion.x_ref
  77.2 4.5 %shard_map.80 = bf16[2,24,1,8,4096]{4,3,2,1,0:T(8,128)(2,1)} custom-call(bf16[24,1,8,4096]{3,2,1,0:T(8,128)(2,1)} %bitcast_select_fusion.x_ref), custom_call_target="tpu_custom_call" | custom-call | tf_op jit(solution)/shard_map/pallas_call | solution.py:101
  81.7 0.0 copy-done.7
  81.7 0.0 copy-done.9
  81.7 0.0 copy-start.15
  81.7 4.1 %copy_select_fusion.1 = bf16[2,4,3,2,8,4096]{5,4,0,1,2,3:T(8,128)(2,1)S(1)} fusion(bf16[2,4,3,2,8,4096]{5,4,3,2,1,0:T(8,128)(2,1)} %bitcast.143, pred[2]{0:T(512)(128)(4,1)S(1)} %iota_compare_fusion.4, pred[4]{0:T(512)(128)(4,1)S(1)} %iota_compare_fusion.3, bf16[3,2,8,4096]{3,2,1,0:T(8,128)(2,1)S(1)} %bitcast_select_fusion.4, ...), kind=kLoop, calls=%fused_computation.6 | loop fusion | flops 2359296 | bytes 8257542 | tf_op jit(solution)/shard_map/jit(_where)/select_n | solution.py:112
  85.8 0.0 copy-done.15
  85.8 0.0 copy-start.5
  85.8 1.0 fusion.16
  86.8 0.1 copy.51
  86.9 0.1 copy.49
  87.0 0.0 copy-done.5
  87.1 0.7 fusion.41
  87.8 0.2 fusion.26
  88.0 0.4 fusion.20
  88.3 0.3 fusion.27
  88.6 1.6 fusion.21
  90.2 0.8 copy.62
  91.1 0.2 copy.53
  91.2 0.1 stack.7
  91.4 0.2 copy.54
  91.5 0.1 stack.8
  91.7 2.6 %convolution_bitcast_fusion = f32[2,4,3,2,8,4096]{5,4,0,1,2,3:T(8,128)S(1)} fusion(bf16[4096,2,128,1,1,1,1]{2,1,0,6,5,4,3:T(2,128)(2,1)} %bitcast.164, bf16[2,3,4,2,8,1,128]{6,4,5,3,2,1,0:T(8,128)(2,1)S(1)} %bitcast.162, bf16[2,3,4,2,8,1,128]{6,4,5,3,2,1,0:T(8,128)(2,1)S(1)} %bitcast.161), kind=kOutput, calls=%fused_computation.5 | convolution fusion | flops 805404672 | bytes 8585216 | tf_op jit(solution)/shard_map/bzxwsch,dch->wxzbsd/dot_general | solution.py:145
  94.3 3.4 %copy.58 = f32[2,4,3,2,8,4096]{5,4,3,2,1,0:T(8,128)} copy(f32[2,4,3,2,8,4096]{5,4,0,1,2,3:T(8,128)S(1)} %convolution_bitcast_fusion) | data formatting | bytes 12582912 | tf_op jit(solution)/shard_map/bzxwsch,dch->wxzbsd/transpose | solution.py:145
  97.7 1.1 copy-done.1
  98.8 6.9 %shard_map.81 = f32[2,24,1,8,4096]{4,3,2,1,0:T(8,128)} custom-call(f32[2,24,1,8,4096]{4,3,2,1,0:T(8,128)} %bitcast.141), custom_call_target="tpu_custom_call" | custom-call | tf_op jit(solution)/shard_map/pallas_call | solution.py:101
  105.7 6.3 %fusion.3 = f32[4,3,2,8,4096]{4,3,0,1,2:T(8,128)S(1)} fusion(f32[2,4,3,2,8,4096]{5,4,0,1,2,3:T(8,128)} %copy-done.1, f32[2,4,3,2,8,4096]{5,4,3,2,1,0:T(8,128)} %bitcast.140, pred[2]{0:T(512)(128)(4,1)S(1)} %copy-done.10), kind=kLoop, calls=%fused_computation.4 | loop fusion | flops 2359296 | bytes 15728642 | tf_op jit(solution)/shard_map/reduce_sum | solution.py:148
  112.0 1.9 copy.60
  113.9 39.1 %shard_map.82 = f32[4,6,1,8,4096]{4,3,2,1,0:T(8,128)} custom-call(f32[4,6,1,8,4096]{4,3,2,1,0:T(8,128)} %bitcast.138), custom_call_target="tpu_custom_call" | custom-call | tf_op jit(solution)/shard_map/pallas_call | solution.py:101
  153.0 4.4 %select_reduce_fusion = f32[6,8,4096]{2,1,0:T(8,128)} fusion(f32[4,6,1,8,4096]{4,3,2,1,0:T(8,128)} %bitcast.139, f32[4,6,1,8,4096]{4,3,2,1,0:T(8,128)} %shard_map.82, pred[4]{0:T(512)(128)(4,1)S(1)} %copy-done.8), kind=kLoop, calls=%fused_computation.7 | loop fusion | flops 1376256 | bytes 7077892 | tf_op jit(solution)/shard_map/reduce_sum | solution.py:149
  157.4 29.2 %shard_map.83 = f32[3,2,1,8,4096]{4,3,2,1,0:T(8,128)} custom-call(f32[3,2,1,8,4096]{4,3,2,1,0:T(8,128)} %bitcast.144), custom_call_target="tpu_custom_call" | custom-call | tf_op jit(solution)/shard_map/pallas_call | solution.py:101
  186.6 1.3 fusion.23
  187.9 0.7 bitcast_bitcast_fusion.x_ref
  188.7 12.9 %shard_map.84 = f32[32,2,1,8,128]{4,3,2,1,0:T(8,128)} custom-call(f32[32,2,1,8,128]{4,3,2,1,0:T(8,128)} %bitcast_bitcast_fusion.x_ref), custom_call_target="tpu_custom_call" | custom-call | tf_op jit(solution)/shard_map/pallas_call | solution.py:101
  201.6 1.7 fusion.29
  (19 shorter events, 0.1 us)
Async XLA Ops:
  0.6 44.0 %copy-start = (bf16[1,4096,128]{2,1,0:T(8,128)(2,1)S(1)}, bf16[1,4096,128]{2,1,0:T(8,128)(2,1)}, u32[]{:S(2)}) copy-start(bf16[1,4096,128]{2,1,0:T(8,128)(2,1)} %param.9) | copy-start | bytes 3145732
  0.6 43.8 %copy-start.6 = (bf16[2,1,512,128]{3,2,1,0:T(8,128)(2,1)S(1)}, bf16[2,1,512,128]{3,2,1,0:T(8,128)(2,1)}, u32[]{:S(2)}) copy-start(bf16[2,1,512,128]{3,2,1,0:T(8,128)(2,1)} %param.8) | copy-start | bytes 786436
  0.7 81.0 %copy-start.7 = (pred[4]{0:T(512)(128)(4,1)}, pred[4]{0:T(512)(128)(4,1)S(1)}, u32[]{:S(2)}) copy-start(pred[4]{0:T(512)(128)(4,1)S(1)} %iota_compare_fusion.3) | copy-start | bytes 16
  0.7 51.0 %copy-start.13 = (pred[3]{0:T(512)(128)(4,1)}, pred[3]{0:T(512)(128)(4,1)S(1)}, u32[]{:S(2)}) copy-start(pred[3]{0:T(512)(128)(4,1)S(1)} %iota_compare_fusion.2) | copy-start | bytes 13
  0.8 80.9 %copy-start.9 = (pred[2]{0:T(512)(128)(4,1)}, pred[2]{0:T(512)(128)(4,1)S(1)}, u32[]{:S(2)}) copy-start(pred[2]{0:T(512)(128)(4,1)S(1)} %iota_compare_fusion.4) | copy-start | bytes 10
  0.8 18.9 %copy-start.11 = (pred[32]{0:T(512)(128)(4,1)}, pred[32]{0:T(512)(128)(4,1)S(1)}, u32[]{:S(2)}) copy-start(pred[32]{0:T(512)(128)(4,1)S(1)} %iota_compare_fusion.1) | copy-start | bytes 100
  44.7 7.1 %copy-start.4 = (bf16[3,2,1,8,4096]{4,3,2,1,0:T(8,128)(2,1)S(1)}, bf16[3,2,1,8,4096]{4,3,2,1,0:T(8,128)(2,1)}, u32[]{:S(2)}) copy-start(bf16[3,2,1,8,4096]{4,3,2,1,0:T(8,128)(2,1)} %shard_map.78) | copy-start | bytes 1179652
  74.3 1.4 copy-start.2
  81.7 4.1 %copy-start.15 = (bf16[1,4096,2,128]{3,2,1,0:T(2,128)(2,1)S(1)}, bf16[1,4096,2,128]{3,2,1,0:T(2,128)(2,1)}, u32[]{:S(2)}) copy-start(bf16[1,4096,2,128]{3,2,1,0:T(2,128)(2,1)} %param.10) | copy-start | bytes 6291460
  85.8 1.3 copy-start.5
  94.3 4.5 %copy-start.1 = (f32[2,4,3,2,8,4096]{5,4,0,1,2,3:T(8,128)}, f32[2,4,3,2,8,4096]{5,4,0,1,2,3:T(8,128)S(1)}, u32[]{:S(2)}) copy-start(f32[2,4,3,2,8,4096]{5,4,0,1,2,3:T(8,128)S(1)} %convolution_bitcast_fusion) | copy-start | bytes 18874372
  98.8 6.9 %copy-start.10 = (pred[2]{0:T(512)(128)(4,1)S(1)}, pred[2]{0:T(512)(128)(4,1)}, u32[]{:S(2)}) copy-start(pred[2]{0:T(512)(128)(4,1)} %copy-done.9) | copy-start | bytes 10
  113.9 39.1 %copy-start.8 = (pred[4]{0:T(512)(128)(4,1)S(1)}, pred[4]{0:T(512)(128)(4,1)}, u32[]{:S(2)}) copy-start(pred[4]{0:T(512)(128)(4,1)} %copy-done.7) | copy-start | bytes 16
  157.4 29.2 %copy-start.3 = (f32[6,8,4096]{2,1,0:T(8,128)S(1)}, f32[6,8,4096]{2,1,0:T(8,128)}, u32[]{:S(2)}) copy-start(f32[6,8,4096]{2,1,0:T(8,128)} %select_reduce_fusion) | copy-start | bytes 2359300
  157.4 29.2 %copy-start.14 = (pred[3]{0:T(512)(128)(4,1)S(1)}, pred[3]{0:T(512)(128)(4,1)}, u32[]{:S(2)}) copy-start(pred[3]{0:T(512)(128)(4,1)} %copy-done.13) | copy-start | bytes 13
  186.6 14.9 %copy-start.12 = (pred[32]{0:T(512)(128)(4,1)S(1)}, pred[32]{0:T(512)(128)(4,1)}, u32[]{:S(2)}) copy-start(pred[32]{0:T(512)(128)(4,1)} %copy-done.11) | copy-start | bytes 100

commit v5 on v4

--- a/solution.py
+++ b/solution.py
@@ -92,12 +92,12 @@
     every.wait_recv()
 
 
-def exchange(x, axis, stride, count, cid, gather):
+def exchange(x, axis, stride, count, cid, gather, wire=None):
     block = x.shape if gather else x.shape[1:]
     lead = () if gather else (count,)
     pieces = math.prod(block[:-2])
-    parts = x.reshape(lead + (pieces, -1) + tuple(block[-2:]))
-    out_shape = jax.ShapeDtypeStruct((count,) + parts.shape[len(lead):], x.dtype)
+    parts = x.astype(wire or x.dtype).reshape(lead + (pieces, -1) + tuple(block[-2:]))
+    out_shape = jax.ShapeDtypeStruct((count,) + parts.shape[len(lead):], parts.dtype)
     received = pl.pallas_call(
         functools.partial(_exchange_kernel, axis, stride, count, gather),
         out_shape=out_shape,
@@ -105,7 +105,7 @@
         out_specs=pl.BlockSpec(memory_space=pl.ANY),
         scratch_shapes=[pltpu.SemaphoreType.DMA, pltpu.SemaphoreType.DMA],
         compiler_params=pltpu.CompilerParams(collective_id=cid, has_side_effects=True),
-    )(parts).reshape((count,) + tuple(block))
+    )(parts).reshape((count,) + tuple(block)).astype(x.dtype)
     digit = lax.rem(lax.div(lax.axis_index(axis), stride), count)
     mine = (jnp.arange(count) == digit).reshape((count,) + (1,) * len(block))
     own = x[None] if gather else x
@@ -145,9 +145,9 @@
     layer_grad = jnp.einsum(
         "bzxwsch,dch->wxzbsd", grad_blocks, keyval_w, preferred_element_type=jnp.float32
     )
-    over_core = exchange(layer_grad, "mp", 1, n_core, 4, False).sum(axis=0)
-    over_x = exchange(over_core, "mp", n_core, n_x, 5, False).sum(axis=0)
-    by_heads = exchange(over_x, "mp", n_x * n_core, n_z, 6, False).sum(axis=0)
+    over_core = exchange(layer_grad, "mp", 1, n_core, 4, False, jnp.bfloat16).sum(axis=0)
+    over_x = exchange(over_core, "mp", n_core, n_x, 5, False, jnp.bfloat16).sum(axis=0)
+    by_heads = exchange(over_x, "mp", n_x * n_core, n_z, 6, False, jnp.bfloat16).sum(axis=0)
     split = by_heads.reshape(nb, ns, n_seg, nd).transpose(2, 0, 1, 3)
     d_enc = exchange(split, "segment", 1, n_seg, 7, False).sum(axis=0)
     return (context[:, None], d_enc)

time: 204 us -> 173 us (0.85)
  Pallas kernels: 155 us -> 125 us
  matrix products: 13.5 us -> 16.2 us
  local copies, waits for them, and re-layouts: 11.5 us -> 8.94 us
    pallas_call x8, Pallas kernels: 155 us -> 125 us  [exchange(): pl.pallas_call(functools.partial(_exchange_kernel, axis, stride, count, g...]
    transpose x1 -> x0, local copies, waits for them, and re-layouts: 3.4 us -> none  [local(): jnp.einsum('bzxwsch,dch->wxzbsd', grad_blocks, keyval_w, preferred_elemen...]
    reduce_sum x3, other arithmetic: 12 us -> 9.17 us  [the longest x1 5.1 us: local(): exchange(layer_grad, 'mp', 1, n_core, 4, False, jnp.bfloat16).sum(axis=0)]
    dot_general x1, matrix products: 2.61 us -> 5.28 us  [local(): jnp.einsum('bzxwsch,dch->wxzbsd', grad_blocks, keyval_w, preferred_elemen...]
    convert_element_type x0 -> x2, other arithmetic: none -> 2.16 us  [exchange(): x.astype(wire or x.dtype).reshape(lead + (pieces, -1) + tuple(block[-2:]))]
where the time goes in v5:
time: 173 us; the launch traced here: 172 us
  Pallas kernels  125 us (72%)
  other arithmetic  21.4 us (12%)
  matrix products  16.2 us (9%)
  local copies, waits for them, and re-layouts  8.94 us (5%)
    pallas_call x8, Pallas kernels, exchange(): pl.pallas_call(functools.partial(_exchange_kernel, axis, stride, count, g...  125 us
    dot_general x1, matrix products, local(): jnp.einsum('btd,dh->bth', inputs, query_w, preferred_element_type=jnp.flo...  7.04 us
    select_n x4, other arithmetic, exchange(): return jnp.where(mine, own, received)  6.45 us
    dot_general x1, matrix products, local(): jnp.einsum('bzxwsch,dch->wxzbsd', grad_blocks, keyval_w, preferred_elemen...  5.28 us
    reduce_sum x1, other arithmetic, local(): exchange(layer_grad, 'mp', 1, n_core, 4, False, jnp.bfloat16).sum(axis=0)  5.1 us
    unnamed x32, local copies, waits for them, and re-layouts  3.94 us

profile of v5, /device:TPU:6, one launch (start us, length us, event | category | flops | bytes accessed | tf_op | source)
XLA Modules:
  0.0 172.4 jit_solution(8296915307528806965)
XLA Ops:
  0.6 0.0 copy-start
  0.6 0.0 copy-start.5
  0.7 0.0 copy-start.6
  0.7 0.0 copy-start.10
  0.8 0.0 copy-start.12
  0.8 0.0 copy-start.8
  0.8 0.1 broadcast_in_dim.137
  0.9 0.1 broadcast_in_dim.138
  1.0 0.7 iota_compare_fusion
  1.7 0.1 broadcast_in_dim.142
  1.8 0.1 broadcast_in_dim.143
  1.8 16.8 %shard_map.77 = bf16[32,2,1,8,128]{4,3,2,1,0:T(8,128)(2,1)} custom-call(bf16[2,1,8,128]{3,2,1,0:T(8,128)(2,1)} %bitcast.166), custom_call_target="tpu_custom_call" | custom-call | tf_op jit(solution)/shard_map/pallas_call | solution.py:101
  18.7 1.0 fusion.34
  19.7 0.0 copy-done.8
  19.8 0.7 reshape_reshape.3
  20.5 24.0 %shard_map.78 = bf16[3,2,1,8,4096]{4,3,2,1,0:T(8,128)(2,1)} custom-call(bf16[2,1,8,4096]{3,2,1,0:T(8,128)(2,1)} %bitcast.158), custom_call_target="tpu_custom_call" | custom-call | tf_op jit(solution)/shard_map/pallas_call | solution.py:101
  44.5 0.0 copy-done.5
  44.5 0.1 copy.52
  44.6 0.0 copy-done
  44.7 0.0 copy-start.3
  44.7 7.0 %fusion.14 = bf16[2,512,128]{1,2,0:T(8,128)(2,1)} fusion(bf16[2,1,512,4096]{3,2,1,0:T(8,128)(2,1)} %param.7, bf16[1,4096,128]{2,1,0:T(8,128)(2,1)S(1)} %copy-done), kind=kOutput, calls=%fused_computation.22 | convolution fusion | flops 1073872896 | bytes 9699328 | tf_op jit(solution)/shard_map/btd,dh->bth/dot_general | solution.py:120
  51.7 0.0 copy-done.10
  51.7 0.0 copy-done.3
  51.7 0.1 bitcast_select_fusion.4
  51.8 0.8 bitcast_select_fusion.3.x_ref
  52.7 21.6 %shard_map.79 = bf16[4,6,1,8,4096]{4,3,2,1,0:T(8,128)(2,1)} custom-call(bf16[6,1,8,4096]{3,2,1,0:T(8,128)(2,1)} %bitcast_select_fusion.3.x_ref), custom_call_target="tpu_custom_call" | custom-call | tf_op jit(solution)/shard_map/pallas_call | solution.py:101
  74.3 0.0 copy-start.2
  74.3 0.2 broadcast_in_dim.136
  74.5 1.2 copy-done.2
  75.7 1.4 bitcast_select_fusion.1.x_ref
  77.2 4.5 %shard_map.80 = bf16[2,24,1,8,4096]{4,3,2,1,0:T(8,128)(2,1)} custom-call(bf16[24,1,8,4096]{3,2,1,0:T(8,128)(2,1)} %bitcast_select_fusion.1.x_ref), custom_call_target="tpu_custom_call" | custom-call | tf_op jit(solution)/shard_map/pallas_call | solution.py:101
  81.7 0.0 copy-start.14
  81.7 4.1 %copy_select_fusion = bf16[2,4,3,2,8,4096]{5,4,0,1,2,3:T(8,128)(2,1)S(1)} fusion(bf16[2,4,3,2,8,4096]{5,4,3,2,1,0:T(8,128)(2,1)} %bitcast.144, pred[2]{0:T(512)(128)(4,1)S(1)} %iota_compare_fusion.4, pred[4]{0:T(512)(128)(4,1)S(1)} %iota_compare_fusion.3, bf16[3,2,8,4096]{3,2,1,0:T(8,128)(2,1)S(1)} %bitcast_select_fusion.4, ...), kind=kLoop, calls=%fused_computation.6 | loop fusion | flops 2359296 | bytes 8257542 | tf_op jit(solution)/shard_map/jit(_where)/select_n | solution.py:112
  85.8 0.0 copy-start.4
  85.8 1.0 fusion.17
  86.8 0.1 copy.51
  86.9 0.1 copy.49
  87.0 0.0 copy-done.4
  87.1 0.7 fusion.42
  87.8 0.2 fusion.27
  88.0 0.4 fusion.21
  88.3 0.3 fusion.28
  88.6 1.6 fusion.22
  90.2 0.8 copy.62
  91.1 0.2 copy.53
  91.2 0.1 stack.7
  91.4 0.2 copy.54
  91.5 0.1 stack.8
  91.7 5.3 %bitcast_convert_fusion = (bf16[2,4,3,2,8,4096]{5,4,0,1,2,3:T(8,128)(2,1)S(1)}, f32[2,3,4,2,8,4096,1]{5,4,6,3,2,1,0:T(8,128)}) fusion(bf16[4096,2,128,1,1,1,1]{2,1,0,6,5,4,3:T(2,128)(2,1)} %bitcast.167, bf16[2,3,4,2,8,1,128]{6,4,5,3,2,1,0:T(8,128)(2,1)S(1)} %bitcast.165, bf16[2,3,4,2,8,1,128]{6,4,5,3,2,1,0:T(8,128)(2,1)S(1)} %bitcast.164), kind=kOutput, calls=%fused_computation.4 | convolution fusion | flops 806977536 | bytes 11730944 | tf_op jit(solution)/shard_map/bzxwsch,dch->wxzbsd/dot_general | solution.py:145
  96.9 2.0 %copy.58 = bf16[2,4,3,2,8,4096]{5,4,3,2,1,0:T(8,128)(2,1)} copy(bf16[2,4,3,2,8,4096]{5,4,0,1,2,3:T(8,128)(2,1)S(1)} %get-tuple-element.16) | data formatting | bytes 6291456 | tf_op jit(solution)/shard_map/convert_element_type | solution.py:99
  98.9 4.6 %shard_map.81 = bf16[2,24,1,8,4096]{4,3,2,1,0:T(8,128)(2,1)} custom-call(bf16[2,24,1,8,4096]{4,3,2,1,0:T(8,128)(2,1)} %bitcast.145), custom_call_target="tpu_custom_call" | custom-call | tf_op jit(solution)/shard_map/pallas_call | solution.py:101
  103.6 0.0 copy-done.13
  103.6 5.1 %fusion.3 = f32[4,3,2,8,4096]{4,3,0,1,2:T(8,128)S(1)} fusion(f32[2,3,4,2,8,4096,1]{5,4,6,3,2,1,0:T(8,128)} %get-tuple-element.17, pred[2]{0:T(512)(128)(4,1)S(1)} %copy-done.13, bf16[2,4,3,2,8,4096]{5,4,3,2,1,0:T(8,128)(2,1)} %bitcast.146), kind=kLoop, calls=%fused_computation.5 | loop fusion | flops 3932160 | bytes 12582914 | tf_op jit(solution)/shard_map/reduce_sum | solution.py:148
  108.7 0.2 copy.60
  108.9 1.7 copy-done.1
  110.6 1.4 convert_element_type.85.x_ref
  111.9 22.3 %shard_map.82 = bf16[4,6,1,8,4096]{4,3,2,1,0:T(8,128)(2,1)} custom-call(bf16[4,6,1,8,4096]{4,3,2,1,0:T(8,128)(2,1)} %convert_element_type.85.x_ref), custom_call_target="tpu_custom_call" | custom-call | tf_op jit(solution)/shard_map/pallas_call | solution.py:101
  134.2 2.9 %select_reduce_fusion = f32[6,8,4096]{2,1,0:T(8,128)S(1)} fusion(f32[4,6,1,8,4096]{4,3,2,1,0:T(8,128)} %bitcast.142, bf16[4,6,1,8,4096]{4,3,2,1,0:T(8,128)(2,1)} %shard_map.82, pred[4]{0:T(512)(128)(4,1)S(1)} %copy-done.7), kind=kLoop, calls=%fused_computation.7 | loop fusion | flops 2162688 | bytes 5505028 | tf_op jit(solution)/shard_map/reduce_sum | solution.py:149
  137.1 0.8 convert_element_type.87
  137.9 18.0 %shard_map.83 = bf16[3,2,1,8,4096]{4,3,2,1,0:T(8,128)(2,1)} custom-call(bf16[3,2,1,8,4096]{4,3,2,1,0:T(8,128)(2,1)} %bitcast.153), custom_call_target="tpu_custom_call" | custom-call | tf_op jit(solution)/shard_map/pallas_call | solution.py:101
  155.9 1.2 fusion.24
  157.1 0.7 bitcast_bitcast_fusion.x_ref
  157.8 13.0 %shard_map.84 = f32[32,2,1,8,128]{4,3,2,1,0:T(8,128)} custom-call(f32[32,2,1,8,128]{4,3,2,1,0:T(8,128)} %bitcast_bitcast_fusion.x_ref), custom_call_target="tpu_custom_call" | custom-call | tf_op jit(solution)/shard_map/pallas_call | solution.py:101
  170.8 1.7 fusion.30
  (19 shorter events, 0.1 us)
Async XLA Ops:
  0.6 44.0 %copy-start = (bf16[1,4096,128]{2,1,0:T(8,128)(2,1)S(1)}, bf16[1,4096,128]{2,1,0:T(8,128)(2,1)}, u32[]{:S(2)}) copy-start(bf16[1,4096,128]{2,1,0:T(8,128)(2,1)} %param.9) | copy-start | bytes 3145732
  0.6 43.8 %copy-start.5 = (bf16[2,1,512,128]{3,2,1,0:T(8,128)(2,1)S(1)}, bf16[2,1,512,128]{3,2,1,0:T(8,128)(2,1)}, u32[]{:S(2)}) copy-start(bf16[2,1,512,128]{3,2,1,0:T(8,128)(2,1)} %param.8) | copy-start | bytes 786436
  0.7 81.0 %copy-start.6 = (pred[4]{0:T(512)(128)(4,1)}, pred[4]{0:T(512)(128)(4,1)S(1)}, u32[]{:S(2)}) copy-start(pred[4]{0:T(512)(128)(4,1)S(1)} %iota_compare_fusion.3) | copy-start | bytes 16
  0.7 51.0 %copy-start.10 = (pred[3]{0:T(512)(128)(4,1)}, pred[3]{0:T(512)(128)(4,1)S(1)}, u32[]{:S(2)}) copy-start(pred[3]{0:T(512)(128)(4,1)S(1)} %iota_compare_fusion.2) | copy-start | bytes 13
  0.8 80.9 %copy-start.12 = (pred[2]{0:T(512)(128)(4,1)}, pred[2]{0:T(512)(128)(4,1)S(1)}, u32[]{:S(2)}) copy-start(pred[2]{0:T(512)(128)(4,1)S(1)} %iota_compare_fusion.4) | copy-start | bytes 10
  0.8 18.9 %copy-start.8 = (pred[32]{0:T(512)(128)(4,1)}, pred[32]{0:T(512)(128)(4,1)S(1)}, u32[]{:S(2)}) copy-start(pred[32]{0:T(512)(128)(4,1)S(1)} %iota_compare_fusion.1) | copy-start | bytes 100
  44.7 7.1 %copy-start.3 = (bf16[3,2,1,8,4096]{4,3,2,1,0:T(8,128)(2,1)S(1)}, bf16[3,2,1,8,4096]{4,3,2,1,0:T(8,128)(2,1)}, u32[]{:S(2)}) copy-start(bf16[3,2,1,8,4096]{4,3,2,1,0:T(8,128)(2,1)} %shard_map.78) | copy-start | bytes 1179652
  74.3 1.4 copy-start.2
  81.7 4.1 %copy-start.14 = (bf16[1,4096,2,128]{3,2,1,0:T(2,128)(2,1)S(1)}, bf16[1,4096,2,128]{3,2,1,0:T(2,128)(2,1)}, u32[]{:S(2)}) copy-start(bf16[1,4096,2,128]{3,2,1,0:T(2,128)(2,1)} %param.10) | copy-start | bytes 6291460
  85.8 1.3 copy-start.4
  98.9 4.6 %copy-start.13 = (pred[2]{0:T(512)(128)(4,1)S(1)}, pred[2]{0:T(512)(128)(4,1)}, u32[]{:S(2)}) copy-start(pred[2]{0:T(512)(128)(4,1)} %copy-done.12) | copy-start | bytes 10
  108.9 1.7 copy-start.1
  111.9 22.3 %copy-start.7 = (pred[4]{0:T(512)(128)(4,1)S(1)}, pred[4]{0:T(512)(128)(4,1)}, u32[]{:S(2)}) copy-start(pred[4]{0:T(512)(128)(4,1)} %copy-done.6) | copy-start | bytes 16
  137.1 18.8 %copy-start.11 = (pred[3]{0:T(512)(128)(4,1)S(1)}, pred[3]{0:T(512)(128)(4,1)}, u32[]{:S(2)}) copy-start(pred[3]{0:T(512)(128)(4,1)} %copy-done.10) | copy-start | bytes 13
  137.9 32.9 %copy-start.9 = (pred[32]{0:T(512)(128)(4,1)S(1)}, pred[32]{0:T(512)(128)(4,1)}, u32[]{:S(2)}) copy-start(pred[32]{0:T(512)(128)(4,1)} %copy-done.8) | copy-start | bytes 100

commit v6 on v5

--- a/solution.py
+++ b/solution.py
@@ -48,7 +48,7 @@
     return (context.reshape(num_batch, num_tgt, width), dkeyval)
 
 
-def _exchange_kernel(axis, stride, count, gather, x_ref, y_ref, send_sem, recv_sem):
+def _exchange_kernel(axis, stride, count, gather, lanes, x_ref, y_ref, send_sem, recv_sem):
     me = lax.axis_index(axis)
     digit = lax.rem(lax.div(me, stride), count)
     base = me - digit * stride
@@ -64,14 +64,17 @@
     lax.fori_loop(1, count, greet, 0)
     pl.semaphore_wait(barrier, count - 1)
 
+    width = y_ref.shape[-1] // lanes
+
     def send(i, carry):
-        k = 1 + lax.div(i, pieces)
-        p = lax.rem(i, pieces)
+        k = 1 + lax.div(i, pieces * lanes)
+        p = lax.rem(lax.div(i, lanes), pieces)
+        cols = pl.ds(pl.multiple_of(lax.rem(i, lanes) * width, width), width)
         slot = lax.rem(digit + k, count)
-        block = x_ref.at[p] if gather else x_ref.at[slot, p]
+        block = x_ref.at[p, :, :, cols] if gather else x_ref.at[slot, p, :, :, cols]
         pltpu.make_async_remote_copy(
             src_ref=block,
-            dst_ref=y_ref.at[digit, p],
+            dst_ref=y_ref.at[digit, p, :, :, cols],
             send_sem=send_sem,
             recv_sem=recv_sem,
             device_id={axis: base + slot * stride},
@@ -79,7 +82,7 @@
         ).start()
         return carry
 
-    lax.fori_loop(0, (count - 1) * pieces, send, 0)
+    lax.fori_loop(0, (count - 1) * pieces * lanes, send, 0)
     every = pltpu.make_async_remote_copy(
         src_ref=y_ref.at[pl.ds(0, count - 1)],
         dst_ref=y_ref.at[pl.ds(0, count - 1)],
@@ -92,14 +95,14 @@
     every.wait_recv()
 
 
-def exchange(x, axis, stride, count, cid, gather, wire=None):
+def exchange(x, axis, stride, count, cid, gather, wire=None, lanes=1):
     block = x.shape if gather else x.shape[1:]
     lead = () if gather else (count,)
     pieces = math.prod(block[:-2])
     parts = x.astype(wire or x.dtype).reshape(lead + (pieces, -1) + tuple(block[-2:]))
     out_shape = jax.ShapeDtypeStruct((count,) + parts.shape[len(lead):], parts.dtype)
     received = pl.pallas_call(
-        functools.partial(_exchange_kernel, axis, stride, count, gather),
+        functools.partial(_exchange_kernel, axis, stride, count, gather, lanes),
         out_shape=out_shape,
         in_specs=[pl.BlockSpec(memory_space=pl.ANY)],
         out_specs=pl.BlockSpec(memory_space=pl.ANY),
@@ -128,8 +131,8 @@
     n_z = n_mp // (n_core * n_x)
     by_feature = exchange(enc_out, "segment", 1, n_seg, 0, True)
     features = by_feature.transpose(1, 2, 0, 3).reshape(nb, ns, n_seg * nd)
-    by_z = exchange(features, "mp", n_x * n_core, n_z, 1, True)
-    by_x = exchange(by_z, "mp", n_core, n_x, 2, True)
+    by_z = exchange(features, "mp", n_x * n_core, n_z, 1, True, lanes=8)
+    by_x = exchange(by_z, "mp", n_core, n_x, 2, True, lanes=4)
     by_core = exchange(by_x, "mp", 1, n_core, 3, True)
     encoder = by_core.transpose(3, 2, 1, 0, 4, 5).reshape(nb, n_mp * ns, n_seg * nd)
     keyval = jnp.einsum(
@@ -146,8 +149,8 @@
         "bzxwsch,dch->wxzbsd", grad_blocks, keyval_w, preferred_element_type=jnp.float32
     )
     over_core = exchange(layer_grad, "mp", 1, n_core, 4, False, jnp.bfloat16).sum(axis=0)
-    over_x = exchange(over_core, "mp", n_core, n_x, 5, False, jnp.bfloat16).sum(axis=0)
-    by_heads = exchange(over_x, "mp", n_x * n_core, n_z, 6, False, jnp.bfloat16).sum(axis=0)
+    over_x = exchange(over_core, "mp", n_core, n_x, 5, False, jnp.bfloat16, 4).sum(axis=0)
+    by_heads = exchange(over_x, "mp", n_x * n_core, n_z, 6, False, jnp.bfloat16, 8).sum(axis=0)
     split = by_heads.reshape(nb, ns, n_seg, nd).transpose(2, 0, 1, 3)
     d_enc = exchange(split, "segment", 1, n_seg, 7, False).sum(axis=0)
     return (context[:, None], d_enc)

time: 173 us -> 174 us (level)
  no operation moved by 1% of the time
where the time goes in v6:
time: 174 us; the launch traced here: 173 us
  Pallas kernels  125 us (72%)
  other arithmetic  21.4 us (12%)
  matrix products  16.2 us (9%)
  local copies, waits for them, and re-layouts  8.94 us (5%)
    pallas_call x8, Pallas kernels, exchange(): pl.pallas_call(functools.partial(_exchange_kernel, axis, stride, count, g...  125 us
    dot_general x1, matrix products, local(): jnp.einsum('btd,dh->bth', inputs, query_w, preferred_element_type=jnp.flo...  7.04 us
    select_n x4, other arithmetic, exchange(): return jnp.where(mine, own, received)  6.45 us
    dot_general x1, matrix products, local(): jnp.einsum('bzxwsch,dch->wxzbsd', grad_blocks, keyval_w, preferred_elemen...  5.28 us
    reduce_sum x1, other arithmetic, local(): exchange(layer_grad, 'mp', 1, n_core, 4, False, jnp.bfloat16).sum(axis=0)  5.1 us
    unnamed x32, local copies, waits for them, and re-layouts  3.94 us

profile of v6, /device:TPU:6, one launch (start us, length us, event | category | flops | bytes accessed | tf_op | source)
XLA Modules:
  0.0 172.8 jit_solution(17044074198165615530)
XLA Ops:
  0.6 0.0 copy-start
  0.6 0.0 copy-start.5
  0.7 0.0 copy-start.6
  0.7 0.0 copy-start.10
  0.8 0.0 copy-start.12
  0.8 0.0 copy-start.8
  0.8 0.1 broadcast_in_dim.137
  0.9 0.1 broadcast_in_dim.138
  1.0 0.7 iota_compare_fusion
  1.7 0.1 broadcast_in_dim.142
  1.8 0.1 broadcast_in_dim.143
  1.8 16.8 %shard_map.77 = bf16[32,2,1,8,128]{4,3,2,1,0:T(8,128)(2,1)} custom-call(bf16[2,1,8,128]{3,2,1,0:T(8,128)(2,1)} %bitcast.166), custom_call_target="tpu_custom_call" | custom-call | tf_op jit(solution)/shard_map/pallas_call | solution.py:104
  18.7 1.0 fusion.34
  19.7 0.0 copy-done.8
  19.8 0.7 reshape_reshape.3
  20.5 24.0 %shard_map.78 = bf16[3,2,1,8,4096]{4,3,2,1,0:T(8,128)(2,1)} custom-call(bf16[2,1,8,4096]{3,2,1,0:T(8,128)(2,1)} %bitcast.158), custom_call_target="tpu_custom_call" | custom-call | tf_op jit(solution)/shard_map/pallas_call | solution.py:104
  44.5 0.0 copy-done.5
  44.5 0.1 copy.52
  44.6 0.0 copy-done
  44.7 0.0 copy-start.3
  44.7 7.0 %fusion.14 = bf16[2,512,128]{1,2,0:T(8,128)(2,1)} fusion(bf16[2,1,512,4096]{3,2,1,0:T(8,128)(2,1)} %param.7, bf16[1,4096,128]{2,1,0:T(8,128)(2,1)S(1)} %copy-done), kind=kOutput, calls=%fused_computation.22 | convolution fusion | flops 1073872896 | bytes 9699328 | tf_op jit(solution)/shard_map/btd,dh->bth/dot_general | solution.py:123
  51.7 0.0 copy-done.10
  51.7 0.0 copy-done.3
  51.7 0.1 bitcast_select_fusion.4
  51.8 0.8 bitcast_select_fusion.3.x_ref
  52.7 21.7 %shard_map.79 = bf16[4,6,1,8,4096]{4,3,2,1,0:T(8,128)(2,1)} custom-call(bf16[6,1,8,4096]{3,2,1,0:T(8,128)(2,1)} %bitcast_select_fusion.3.x_ref), custom_call_target="tpu_custom_call" | custom-call | tf_op jit(solution)/shard_map/pallas_call | solution.py:104
  74.4 0.2 broadcast_in_dim.136
  74.6 1.2 copy-done.2
  75.8 1.4 bitcast_select_fusion.1.x_ref
  77.3 4.5 %shard_map.80 = bf16[2,24,1,8,4096]{4,3,2,1,0:T(8,128)(2,1)} custom-call(bf16[24,1,8,4096]{3,2,1,0:T(8,128)(2,1)} %bitcast_select_fusion.1.x_ref), custom_call_target="tpu_custom_call" | custom-call | tf_op jit(solution)/shard_map/pallas_call | solution.py:104
  81.8 0.0 copy-done.6
  81.8 0.0 copy-done.12
  81.8 0.0 copy-start.14
  81.8 4.1 %copy_select_fusion = bf16[2,4,3,2,8,4096]{5,4,0,1,2,3:T(8,128)(2,1)S(1)} fusion(bf16[2,4,3,2,8,4096]{5,4,3,2,1,0:T(8,128)(2,1)} %bitcast.144, pred[2]{0:T(512)(128)(4,1)S(1)} %iota_compare_fusion.4, pred[4]{0:T(512)(128)(4,1)S(1)} %iota_compare_fusion.3, bf16[3,2,8,4096]{3,2,1,0:T(8,128)(2,1)S(1)} %bitcast_select_fusion.4, ...), kind=kLoop, calls=%fused_computation.6 | loop fusion | flops 2359296 | bytes 8257542 | tf_op jit(solution)/shard_map/jit(_where)/select_n | solution.py:115
  85.9 0.0 copy-start.4
  85.9 1.0 fusion.17
  86.9 0.1 copy.51
  87.0 0.1 copy.49
  87.2 0.7 fusion.42
  87.8 0.2 fusion.27
  88.1 0.4 fusion.21
  88.4 0.3 fusion.28
  88.7 1.6 fusion.22
  90.3 0.8 copy.62
  91.1 0.2 copy.53
  91.3 0.1 stack.7
  91.4 0.2 copy.54
  91.6 0.1 stack.8
  91.7 5.3 %bitcast_convert_fusion = (bf16[2,4,3,2,8,4096]{5,4,0,1,2,3:T(8,128)(2,1)S(1)}, f32[2,3,4,2,8,4096,1]{5,4,6,3,2,1,0:T(8,128)}) fusion(bf16[4096,2,128,1,1,1,1]{2,1,0,6,5,4,3:T(2,128)(2,1)} %bitcast.167, bf16[2,3,4,2,8,1,128]{6,4,5,3,2,1,0:T(8,128)(2,1)S(1)} %bitcast.165, bf16[2,3,4,2,8,1,128]{6,4,5,3,2,1,0:T(8,128)(2,1)S(1)} %bitcast.164), kind=kOutput, calls=%fused_computation.4 | convolution fusion | flops 806977536 | bytes 11730944 | tf_op jit(solution)/shard_map/bzxwsch,dch->wxzbsd/dot_general | solution.py:148
  97.0 2.0 %copy.58 = bf16[2,4,3,2,8,4096]{5,4,3,2,1,0:T(8,128)(2,1)} copy(bf16[2,4,3,2,8,4096]{5,4,0,1,2,3:T(8,128)(2,1)S(1)} %get-tuple-element.16) | data formatting | bytes 6291456 | tf_op jit(solution)/shard_map/convert_element_type | solution.py:102
  99.0 4.6 %shard_map.81 = bf16[2,24,1,8,4096]{4,3,2,1,0:T(8,128)(2,1)} custom-call(bf16[2,24,1,8,4096]{4,3,2,1,0:T(8,128)(2,1)} %bitcast.145), custom_call_target="tpu_custom_call" | custom-call | tf_op jit(solution)/shard_map/pallas_call | solution.py:104
  103.7 5.1 %fusion.3 = f32[4,3,2,8,4096]{4,3,0,1,2:T(8,128)S(1)} fusion(f32[2,3,4,2,8,4096,1]{5,4,6,3,2,1,0:T(8,128)} %get-tuple-element.17, pred[2]{0:T(512)(128)(4,1)S(1)} %copy-done.13, bf16[2,4,3,2,8,4096]{5,4,3,2,1,0:T(8,128)(2,1)} %bitcast.146), kind=kLoop, calls=%fused_computation.5 | loop fusion | flops 3932160 | bytes 12582914 | tf_op jit(solution)/shard_map/reduce_sum | solution.py:151
  108.8 0.2 copy.60
  109.0 1.7 copy-done.1
  110.6 1.4 convert_element_type.85.x_ref
  112.0 22.4 %shard_map.82 = bf16[4,6,1,8,4096]{4,3,2,1,0:T(8,128)(2,1)} custom-call(bf16[4,6,1,8,4096]{4,3,2,1,0:T(8,128)(2,1)} %convert_element_type.85.x_ref), custom_call_target="tpu_custom_call" | custom-call | tf_op jit(solution)/shard_map/pallas_call | solution.py:104
  134.5 0.0 copy-done.7
  134.5 2.9 %select_reduce_fusion = f32[6,8,4096]{2,1,0:T(8,128)S(1)} fusion(f32[4,6,1,8,4096]{4,3,2,1,0:T(8,128)} %bitcast.142, bf16[4,6,1,8,4096]{4,3,2,1,0:T(8,128)(2,1)} %shard_map.82, pred[4]{0:T(512)(128)(4,1)S(1)} %copy-done.7), kind=kLoop, calls=%fused_computation.7 | loop fusion | flops 2162688 | bytes 5505028 | tf_op jit(solution)/shard_map/reduce_sum | solution.py:152
  137.4 0.8 convert_element_type.87
  138.2 18.1 %shard_map.83 = bf16[3,2,1,8,4096]{4,3,2,1,0:T(8,128)(2,1)} custom-call(bf16[3,2,1,8,4096]{4,3,2,1,0:T(8,128)(2,1)} %bitcast.153), custom_call_target="tpu_custom_call" | custom-call | tf_op jit(solution)/shard_map/pallas_call | solution.py:104
  156.2 1.2 fusion.24
  157.4 0.7 bitcast_bitcast_fusion.x_ref
  158.1 13.0 %shard_map.84 = f32[32,2,1,8,128]{4,3,2,1,0:T(8,128)} custom-call(f32[32,2,1,8,128]{4,3,2,1,0:T(8,128)} %bitcast_bitcast_fusion.x_ref), custom_call_target="tpu_custom_call" | custom-call | tf_op jit(solution)/shard_map/pallas_call | solution.py:104
  171.1 1.7 fusion.30
  (19 shorter events, 0.1 us)
Async XLA Ops:
  0.6 44.0 %copy-start = (bf16[1,4096,128]{2,1,0:T(8,128)(2,1)S(1)}, bf16[1,4096,128]{2,1,0:T(8,128)(2,1)}, u32[]{:S(2)}) copy-start(bf16[1,4096,128]{2,1,0:T(8,128)(2,1)} %param.9) | copy-start | bytes 3145732
  0.6 43.8 %copy-start.5 = (bf16[2,1,512,128]{3,2,1,0:T(8,128)(2,1)S(1)}, bf16[2,1,512,128]{3,2,1,0:T(8,128)(2,1)}, u32[]{:S(2)}) copy-start(bf16[2,1,512,128]{3,2,1,0:T(8,128)(2,1)} %param.8) | copy-start | bytes 786436
  0.7 81.1 %copy-start.6 = (pred[4]{0:T(512)(128)(4,1)}, pred[4]{0:T(512)(128)(4,1)S(1)}, u32[]{:S(2)}) copy-start(pred[4]{0:T(512)(128)(4,1)S(1)} %iota_compare_fusion.3) | copy-start | bytes 16
  0.7 51.0 %copy-start.10 = (pred[3]{0:T(512)(128)(4,1)}, pred[3]{0:T(512)(128)(4,1)S(1)}, u32[]{:S(2)}) copy-start(pred[3]{0:T(512)(128)(4,1)S(1)} %iota_compare_fusion.2) | copy-start | bytes 13
  0.8 81.0 %copy-start.12 = (pred[2]{0:T(512)(128)(4,1)}, pred[2]{0:T(512)(128)(4,1)S(1)}, u32[]{:S(2)}) copy-start(pred[2]{0:T(512)(128)(4,1)S(1)} %iota_compare_fusion.4) | copy-start | bytes 10
  0.8 18.9 %copy-start.8 = (pred[32]{0:T(512)(128)(4,1)}, pred[32]{0:T(512)(128)(4,1)S(1)}, u32[]{:S(2)}) copy-start(pred[32]{0:T(512)(128)(4,1)S(1)} %iota_compare_fusion.1) | copy-start | bytes 100
  44.7 7.1 %copy-start.3 = (bf16[3,2,1,8,4096]{4,3,2,1,0:T(8,128)(2,1)S(1)}, bf16[3,2,1,8,4096]{4,3,2,1,0:T(8,128)(2,1)}, u32[]{:S(2)}) copy-start(bf16[3,2,1,8,4096]{4,3,2,1,0:T(8,128)(2,1)} %shard_map.78) | copy-start | bytes 1179652
  74.4 1.4 copy-start.2
  81.8 4.1 %copy-start.14 = (bf16[1,4096,2,128]{3,2,1,0:T(2,128)(2,1)S(1)}, bf16[1,4096,2,128]{3,2,1,0:T(2,128)(2,1)}, u32[]{:S(2)}) copy-start(bf16[1,4096,2,128]{3,2,1,0:T(2,128)(2,1)} %param.10) | copy-start | bytes 6291460
  85.9 1.3 copy-start.4
  99.0 4.6 %copy-start.13 = (pred[2]{0:T(512)(128)(4,1)S(1)}, pred[2]{0:T(512)(128)(4,1)}, u32[]{:S(2)}) copy-start(pred[2]{0:T(512)(128)(4,1)} %copy-done.12) | copy-start | bytes 10
  109.0 1.7 copy-start.1
  112.0 22.4 %copy-start.7 = (pred[4]{0:T(512)(128)(4,1)S(1)}, pred[4]{0:T(512)(128)(4,1)}, u32[]{:S(2)}) copy-start(pred[4]{0:T(512)(128)(4,1)} %copy-done.6) | copy-start | bytes 16
  137.4 18.9 %copy-start.11 = (pred[3]{0:T(512)(128)(4,1)S(1)}, pred[3]{0:T(512)(128)(4,1)}, u32[]{:S(2)}) copy-start(pred[3]{0:T(512)(128)(4,1)} %copy-done.10) | copy-start | bytes 13
  138.2 32.9 %copy-start.9 = (pred[32]{0:T(512)(128)(4,1)S(1)}, pred[32]{0:T(512)(128)(4,1)}, u32[]{:S(2)}) copy-start(pred[32]{0:T(512)(128)(4,1)} %copy-done.8) | copy-start | bytes 100

commit v7 on v5

--- a/solution.py
+++ b/solution.py
@@ -126,10 +126,10 @@
     n_core = 2
     n_x = n_mp // (n_core * 3)
     n_z = n_mp // (n_core * n_x)
-    by_feature = exchange(enc_out, "segment", 1, n_seg, 0, True)
-    features = by_feature.transpose(1, 2, 0, 3).reshape(nb, ns, n_seg * nd)
-    by_z = exchange(features, "mp", n_x * n_core, n_z, 1, True)
-    by_x = exchange(by_z, "mp", n_core, n_x, 2, True)
+    by_z = exchange(enc_out, "mp", n_x * n_core, n_z, 0, True)
+    by_seg = exchange(by_z, "segment", 1, n_seg, 1, True)
+    features = by_seg.transpose(1, 2, 3, 0, 4).reshape(n_z, nb, ns, n_seg * nd)
+    by_x = exchange(features, "mp", n_core, n_x, 2, True)
     by_core = exchange(by_x, "mp", 1, n_core, 3, True)
     encoder = by_core.transpose(3, 2, 1, 0, 4, 5).reshape(nb, n_mp * ns, n_seg * nd)
     keyval = jnp.einsum(
@@ -147,9 +147,9 @@
     )
     over_core = exchange(layer_grad, "mp", 1, n_core, 4, False, jnp.bfloat16).sum(axis=0)
     over_x = exchange(over_core, "mp", n_core, n_x, 5, False, jnp.bfloat16).sum(axis=0)
-    by_heads = exchange(over_x, "mp", n_x * n_core, n_z, 6, False, jnp.bfloat16).sum(axis=0)
-    split = by_heads.reshape(nb, ns, n_seg, nd).transpose(2, 0, 1, 3)
-    d_enc = exchange(split, "segment", 1, n_seg, 7, False).sum(axis=0)
+    split = over_x.reshape(n_z, nb, ns, n_seg, nd).transpose(3, 0, 1, 2, 4)
+    by_layer = exchange(split, "segment", 1, n_seg, 6, False, jnp.bfloat16).sum(axis=0)
+    d_enc = exchange(by_layer, "mp", n_x * n_core, n_z, 7, False).sum(axis=0)
     return (context[:, None], d_enc)
 
 

time: 173 us -> 170 us (0.983)
  Pallas kernels: 125 us -> 118 us
  local copies, waits for them, and re-layouts: 8.94 us -> 11.2 us
    pallas_call x8, Pallas kernels: 125 us -> 118 us  [exchange(): pl.pallas_call(functools.partial(_exchange_kernel, axis, stride, count, g...]
    unnamed x32 -> x29, local copies, waits for them, and re-layouts: 3.94 us -> 5.01 us
where the time goes in v7:
time: 170 us; the launch traced here: 169 us
  Pallas kernels  118 us (69%)
  other arithmetic  22.6 us (13%)
  matrix products  16.2 us (10%)
  local copies, waits for them, and re-layouts  11.2 us (7%)
    pallas_call x8, Pallas kernels, exchange(): pl.pallas_call(functools.partial(_exchange_kernel, axis, stride, count, g...  118 us
    select_n x4, other arithmetic, exchange(): return jnp.where(mine, own, received)  7.67 us
    dot_general x1, matrix products, local(): jnp.einsum('btd,dh->bth', inputs, query_w, preferred_element_type=jnp.flo...  6.99 us
    dot_general x1, matrix products, local(): jnp.einsum('bzxwsch,dch->wxzbsd', grad_blocks, keyval_w, preferred_elemen...  5.28 us
    reduce_sum x1, other arithmetic, local(): exchange(layer_grad, 'mp', 1, n_core, 4, False, jnp.bfloat16).sum(axis=0)  5.1 us
    unnamed x29, local copies, waits for them, and re-layouts  5.01 us

profile of v7, /device:TPU:6, one launch (start us, length us, event | category | flops | bytes accessed | tf_op | source)
XLA Modules:
  0.0 168.8 jit_solution(10018832928125532975)
XLA Ops:
  0.6 0.0 copy-start
  0.7 0.0 copy-start.4
  0.7 0.0 copy-start.6
  0.7 0.0 copy-start.8
  0.8 0.0 copy-start.10
  0.8 0.1 broadcast_in_dim.135
  0.9 0.1 broadcast_in_dim.136
  0.9 0.8 iota_compare_fusion
  1.7 0.1 broadcast_in_dim.142
  1.8 0.1 broadcast_in_dim.143
  1.9 18.3 %shard_map.77 = bf16[3,2,1,8,128]{4,3,2,1,0:T(8,128)(2,1)} custom-call(bf16[2,1,8,128]{3,2,1,0:T(8,128)(2,1)} %bitcast.150), custom_call_target="tpu_custom_call" | custom-call | tf_op jit(solution)/shard_map/pallas_call | solution.py:101
  20.2 0.8 bitcast_select_fusion.6
  21.0 0.7 broadcast_in_dim.133
  21.7 1.4 bitcast_select_fusion.5.x_ref
  23.1 1.1 copy.50
  24.2 0.0 copy-done
  24.2 7.0 %fusion.14 = bf16[2,512,128]{1,2,0:T(8,128)(2,1)} fusion(bf16[2,1,512,4096]{3,2,1,0:T(8,128)(2,1)} %param.7, bf16[1,4096,128]{2,1,0:T(8,128)(2,1)S(1)} %copy-done), kind=kOutput, calls=%fused_computation.22 | convolution fusion | flops 1073872896 | bytes 9699328 | tf_op jit(solution)/shard_map/btd,dh->bth/dot_general | solution.py:120
  31.1 0.0 copy-done.6
  31.2 19.6 %shard_map.78 = bf16[32,6,1,8,128]{4,3,2,1,0:T(8,128)(2,1)} custom-call(bf16[6,1,8,128]{3,2,1,0:T(8,128)(2,1)} %bitcast_select_fusion.5.x_ref), custom_call_target="tpu_custom_call" | custom-call | tf_op jit(solution)/shard_map/pallas_call | solution.py:101
  50.8 1.1 fusion.29
  51.9 0.2 broadcast_in_dim.139
  52.0 0.9 reshape_reshape.3.x_ref
  52.9 21.8 %shard_map.79 = bf16[4,6,1,8,4096]{4,3,2,1,0:T(8,128)(2,1)} custom-call(bf16[6,1,8,4096]{3,2,1,0:T(8,128)(2,1)} %reshape_reshape.3.x_ref), custom_call_target="tpu_custom_call" | custom-call | tf_op jit(solution)/shard_map/pallas_call | solution.py:101
  74.8 0.0 copy-start.2
  74.8 0.2 broadcast_in_dim.140
  74.9 1.2 copy-done.2
  76.2 1.4 bitcast_select_fusion.1.x_ref
  77.6 4.5 %shard_map.80 = bf16[2,24,1,8,4096]{4,3,2,1,0:T(8,128)(2,1)} custom-call(bf16[24,1,8,4096]{3,2,1,0:T(8,128)(2,1)} %bitcast_select_fusion.1.x_ref), custom_call_target="tpu_custom_call" | custom-call | tf_op jit(solution)/shard_map/pallas_call | solution.py:101
  82.1 0.0 copy-start.12
  82.1 4.1 %copy_select_fusion = bf16[2,4,3,2,8,4096]{5,4,0,1,2,3:T(8,128)(2,1)S(1)} fusion(bf16[2,4,3,2,8,4096]{5,4,3,2,1,0:T(8,128)(2,1)} %bitcast.126, pred[2]{0:T(512)(128)(4,1)S(1)} %iota_compare_fusion.4, pred[4]{0:T(512)(128)(4,1)S(1)} %iota_compare_fusion.3, bf16[3,2,8,4096]{3,2,1,0:T(8,128)(2,1)S(1)} %broadcast_in_dim.139, ...), kind=kLoop, calls=%fused_computation.6 | loop fusion | flops 2359296 | bytes 8257542 | tf_op jit(solution)/shard_map/jit(_where)/select_n | solution.py:112
  86.2 0.0 copy-start.3
  86.2 1.0 fusion.17
  87.2 0.1 copy.49
  87.4 0.1 copy.47
  87.5 0.7 fusion.40
  88.2 0.2 fusion.27
  88.4 0.4 fusion.21
  88.8 0.3 fusion.28
  89.1 1.6 fusion.22
  90.6 0.8 copy.61
  91.5 0.2 copy.51
  91.7 0.1 stack.7
  91.8 0.2 copy.52
  92.0 0.1 stack.8
  92.1 5.3 %bitcast_convert_fusion = (bf16[2,4,3,2,8,4096]{5,4,0,1,2,3:T(8,128)(2,1)S(1)}, f32[2,3,4,2,8,4096,1]{5,4,6,3,2,1,0:T(8,128)}) fusion(bf16[4096,2,128,1,1,1,1]{2,1,0,6,5,4,3:T(2,128)(2,1)} %bitcast.151, bf16[2,3,4,2,8,1,128]{6,4,5,3,2,1,0:T(8,128)(2,1)S(1)} %bitcast.148, bf16[2,3,4,2,8,1,128]{6,4,5,3,2,1,0:T(8,128)(2,1)S(1)} %bitcast.147), kind=kOutput, calls=%fused_computation.4 | convolution fusion | flops 806977536 | bytes 11730944 | tf_op jit(solution)/shard_map/bzxwsch,dch->wxzbsd/dot_general | solution.py:145
  97.4 2.0 %copy.56 = bf16[2,4,3,2,8,4096]{5,4,3,2,1,0:T(8,128)(2,1)} copy(bf16[2,4,3,2,8,4096]{5,4,0,1,2,3:T(8,128)(2,1)S(1)} %get-tuple-element.14) | data formatting | bytes 6291456 | tf_op jit(solution)/shard_map/convert_element_type | solution.py:99
  99.4 4.6 %shard_map.81 = bf16[2,24,1,8,4096]{4,3,2,1,0:T(8,128)(2,1)} custom-call(bf16[2,24,1,8,4096]{4,3,2,1,0:T(8,128)(2,1)} %bitcast.127), custom_call_target="tpu_custom_call" | custom-call | tf_op jit(solution)/shard_map/pallas_call | solution.py:101
  104.0 5.1 %fusion.3 = f32[4,3,2,8,4096]{4,3,0,1,2:T(8,128)S(1)} fusion(f32[2,3,4,2,8,4096,1]{5,4,6,3,2,1,0:T(8,128)} %get-tuple-element.15, pred[2]{0:T(512)(128)(4,1)S(1)} %copy-done.9, bf16[2,4,3,2,8,4096]{5,4,3,2,1,0:T(8,128)(2,1)} %bitcast.128), kind=kLoop, calls=%fused_computation.5 | loop fusion | flops 3932160 | bytes 12582914 | tf_op jit(solution)/shard_map/reduce_sum | solution.py:148
  109.1 0.2 copy.58
  109.3 1.7 copy-done.1
  111.0 1.4 convert_element_type.75.x_ref
  112.4 22.3 %shard_map.82 = bf16[4,6,1,8,4096]{4,3,2,1,0:T(8,128)(2,1)} custom-call(bf16[4,6,1,8,4096]{4,3,2,1,0:T(8,128)(2,1)} %convert_element_type.75.x_ref), custom_call_target="tpu_custom_call" | custom-call | tf_op jit(solution)/shard_map/pallas_call | solution.py:101
  134.6 0.0 copy-done.5
  134.6 2.9 %select_reduce_fusion = f32[6,8,4096]{2,1,0:T(8,128)S(1)} fusion(f32[4,6,1,8,4096]{4,3,2,1,0:T(8,128)} %bitcast.124, bf16[4,6,1,8,4096]{4,3,2,1,0:T(8,128)(2,1)} %shard_map.82, pred[4]{0:T(512)(128)(4,1)S(1)} %copy-done.5), kind=kLoop, calls=%fused_computation.7 | loop fusion | flops 2162688 | bytes 5505028 | tf_op jit(solution)/shard_map/reduce_sum | solution.py:149
  137.6 0.1 copy.77
  137.7 0.1 bitcast_convert_fusion.1
  137.8 0.9 copy.59
  138.7 17.9 %shard_map.83 = bf16[32,6,1,8,128]{4,3,2,1,0:T(8,128)(2,1)} custom-call(bf16[32,6,1,8,128]{4,3,2,1,0:T(8,128)(2,1)} %bitcast.137), custom_call_target="tpu_custom_call" | custom-call | tf_op jit(solution)/shard_map/pallas_call | solution.py:101
  156.6 0.0 copy-start.7
  156.6 1.0 bitcast_convert_fusion.2
  157.7 0.0 copy-done.11
  157.7 1.0 fusion.24
  158.7 8.7 %shard_map.84 = f32[3,2,1,8,128]{4,3,2,1,0:T(8,128)} custom-call(f32[3,2,1,8,128]{4,3,2,1,0:T(8,128)} %bitcast.145), custom_call_target="tpu_custom_call" | custom-call | tf_op jit(solution)/shard_map/pallas_call | solution.py:101
  167.3 1.4 fusion.33
  (16 shorter events, 0.1 us)
Async XLA Ops:
  0.6 23.5 %copy-start = (bf16[1,4096,128]{2,1,0:T(8,128)(2,1)S(1)}, bf16[1,4096,128]{2,1,0:T(8,128)(2,1)}, u32[]{:S(2)}) copy-start(bf16[1,4096,128]{2,1,0:T(8,128)(2,1)} %param.9) | copy-start | bytes 3145732
  0.7 81.4 %copy-start.4 = (pred[4]{0:T(512)(128)(4,1)}, pred[4]{0:T(512)(128)(4,1)S(1)}, u32[]{:S(2)}) copy-start(pred[4]{0:T(512)(128)(4,1)S(1)} %iota_compare_fusion.3) | copy-start | bytes 16
  0.7 30.4 %copy-start.6 = (pred[3]{0:T(512)(128)(4,1)}, pred[3]{0:T(512)(128)(4,1)S(1)}, u32[]{:S(2)}) copy-start(pred[3]{0:T(512)(128)(4,1)S(1)} %iota_compare_fusion.1) | copy-start | bytes 13
  0.7 81.4 %copy-start.8 = (pred[2]{0:T(512)(128)(4,1)}, pred[2]{0:T(512)(128)(4,1)S(1)}, u32[]{:S(2)}) copy-start(pred[2]{0:T(512)(128)(4,1)S(1)} %iota_compare_fusion.4) | copy-start | bytes 10
  0.8 50.0 %copy-start.10 = (pred[32]{0:T(512)(128)(4,1)}, pred[32]{0:T(512)(128)(4,1)S(1)}, u32[]{:S(2)}) copy-start(pred[32]{0:T(512)(128)(4,1)S(1)} %iota_compare_fusion.2) | copy-start | bytes 100
  74.8 1.4 copy-start.2
  82.1 4.1 %copy-start.12 = (bf16[1,4096,2,128]{3,2,1,0:T(2,128)(2,1)S(1)}, bf16[1,4096,2,128]{3,2,1,0:T(2,128)(2,1)}, u32[]{:S(2)}) copy-start(bf16[1,4096,2,128]{3,2,1,0:T(2,128)(2,1)} %param.10) | copy-start | bytes 6291460
  86.2 1.3 copy-start.3
  99.4 4.6 %copy-start.9 = (pred[2]{0:T(512)(128)(4,1)S(1)}, pred[2]{0:T(512)(128)(4,1)}, u32[]{:S(2)}) copy-start(pred[2]{0:T(512)(128)(4,1)} %copy-done.8) | copy-start | bytes 10
  109.3 1.7 copy-start.1
  112.4 22.3 %copy-start.5 = (pred[4]{0:T(512)(128)(4,1)S(1)}, pred[4]{0:T(512)(128)(4,1)}, u32[]{:S(2)}) copy-start(pred[4]{0:T(512)(128)(4,1)} %copy-done.4) | copy-start | bytes 16
  137.8 19.9 %copy-start.11 = (pred[32]{0:T(512)(128)(4,1)S(1)}, pred[32]{0:T(512)(128)(4,1)}, u32[]{:S(2)}) copy-start(pred[32]{0:T(512)(128)(4,1)} %copy-done.10) | copy-start | bytes 100
  156.6 10.7 %copy-start.7 = (pred[3]{0:T(512)(128)(4,1)S(1)}, pred[3]{0:T(512)(128)(4,1)}, u32[]{:S(2)}) copy-start(pred[3]{0:T(512)(128)(4,1)} %copy-done.6) | copy-start | bytes 13

commit v8 on v7

--- a/solution.py
+++ b/solution.py
@@ -48,66 +48,79 @@
     return (context.reshape(num_batch, num_tgt, width), dkeyval)
 
 
-def _exchange_kernel(axis, stride, count, gather, x_ref, y_ref, send_sem, recv_sem):
+def _exchange_kernel(axis, stride, count, inner, gather, x_ref, y_ref, send_sem, recv_sem):
     me = lax.axis_index(axis)
     digit = lax.rem(lax.div(me, stride), count)
     base = me - digit * stride
+    n_inner = lax.axis_size(inner) if inner else 1
+    mine = digit * n_inner + (lax.axis_index(inner) if inner else 0)
+    total = count * n_inner
     pieces = y_ref.shape[1]
     mesh_ids = pl.DeviceIdType.MESH
+
+    def device_of(slot):
+        where = {axis: base + lax.div(slot, n_inner) * stride}
+        if inner:
+            where[inner] = lax.rem(slot, n_inner)
+        return where
+
     barrier = pltpu.get_barrier_semaphore()
 
     def greet(k, carry):
-        peer = base + lax.rem(digit + k, count) * stride
-        pl.semaphore_signal(barrier, inc=1, device_id={axis: peer}, device_id_type=mesh_ids)
+        slot = lax.rem(mine + k, total)
+        pl.semaphore_signal(barrier, inc=1, device_id=device_of(slot), device_id_type=mesh_ids)
         return carry
 
-    lax.fori_loop(1, count, greet, 0)
-    pl.semaphore_wait(barrier, count - 1)
+    lax.fori_loop(1, total, greet, 0)
+    pl.semaphore_wait(barrier, total - 1)
 
     def send(i, carry):
         k = 1 + lax.div(i, pieces)
         p = lax.rem(i, pieces)
-        slot = lax.rem(digit + k, count)
+        slot = lax.rem(mine + k, total)
         block = x_ref.at[p] if gather else x_ref.at[slot, p]
         pltpu.make_async_remote_copy(
             src_ref=block,
-            dst_ref=y_ref.at[digit, p],
+            dst_ref=y_ref.at[mine, p],
             send_sem=send_sem,
             recv_sem=recv_sem,
-            device_id={axis: base + slot * stride},
+            device_id=device_of(slot),
             device_id_type=mesh_ids,
         ).start()
         return carry
 
-    lax.fori_loop(0, (count - 1) * pieces, send, 0)
+    lax.fori_loop(0, (total - 1) * pieces, send, 0)
     every = pltpu.make_async_remote_copy(
-        src_ref=y_ref.at[pl.ds(0, count - 1)],
-        dst_ref=y_ref.at[pl.ds(0, count - 1)],
+        src_ref=y_ref.at[pl.ds(0, total - 1)],
+        dst_ref=y_ref.at[pl.ds(0, total - 1)],
         send_sem=send_sem,
         recv_sem=recv_sem,
-        device_id={axis: base + lax.rem(digit + 1, count) * stride},
+        device_id=device_of(lax.rem(mine + 1, total)),
         device_id_type=mesh_ids,
     )
     every.wait_send()
     every.wait_recv()
 
 
-def exchange(x, axis, stride, count, cid, gather, wire=None):
+def exchange(x, axis, stride, count, cid, gather, wire=None, inner=None):
+    total = count * (lax.axis_size(inner) if inner else 1)
     block = x.shape if gather else x.shape[1:]
-    lead = () if gather else (count,)
+    lead = () if gather else (total,)
     pieces = math.prod(block[:-2])
     parts = x.astype(wire or x.dtype).reshape(lead + (pieces, -1) + tuple(block[-2:]))
-    out_shape = jax.ShapeDtypeStruct((count,) + parts.shape[len(lead):], parts.dtype)
+    out_shape = jax.ShapeDtypeStruct((total,) + parts.shape[len(lead):], parts.dtype)
     received = pl.pallas_call(
-        functools.partial(_exchange_kernel, axis, stride, count, gather),
+        functools.partial(_exchange_kernel, axis, stride, count, inner, gather),
         out_shape=out_shape,
         in_specs=[pl.BlockSpec(memory_space=pl.ANY)],
         out_specs=pl.BlockSpec(memory_space=pl.ANY),
         scratch_shapes=[pltpu.SemaphoreType.DMA, pltpu.SemaphoreType.DMA],
         compiler_params=pltpu.CompilerParams(collective_id=cid, has_side_effects=True),
-    )(parts).reshape((count,) + tuple(block)).astype(x.dtype)
+    )(parts).reshape((total,) + tuple(block)).astype(x.dtype)
     digit = lax.rem(lax.div(lax.axis_index(axis), stride), count)
-    mine = (jnp.arange(count) == digit).reshape((count,) + (1,) * len(block))
+    if inner:
+        digit = digit * lax.axis_size(inner) + lax.axis_index(inner)
+    mine = (jnp.arange(total) == digit).reshape((total,) + (1,) * len(block))
     own = x[None] if gather else x
     return jnp.where(mine, own, received)
 
@@ -126,9 +139,10 @@
     n_core = 2
     n_x = n_mp // (n_core * 3)
     n_z = n_mp // (n_core * n_x)
-    by_z = exchange(enc_out, "mp", n_x * n_core, n_z, 0, True)
-    by_seg = exchange(by_z, "segment", 1, n_seg, 1, True)
-    features = by_seg.transpose(1, 2, 3, 0, 4).reshape(n_z, nb, ns, n_seg * nd)
+    by_zs = exchange(enc_out, "mp", n_x * n_core, n_z, 0, True, inner="segment")
+    features = (
+        by_zs.reshape(n_z, n_seg, nb, ns, nd).transpose(0, 2, 3, 1, 4).reshape(n_z, nb, ns, n_seg * nd)
+    )
     by_x = exchange(features, "mp", n_core, n_x, 2, True)
     by_core = exchange(by_x, "mp", 1, n_core, 3, True)
     encoder = by_core.transpose(3, 2, 1, 0, 4, 5).reshape(nb, n_mp * ns, n_seg * nd)
@@ -147,9 +161,10 @@
     )
     over_core = exchange(layer_grad, "mp", 1, n_core, 4, False, jnp.bfloat16).sum(axis=0)
     over_x = exchange(over_core, "mp", n_core, n_x, 5, False, jnp.bfloat16).sum(axis=0)
-    split = over_x.reshape(n_z, nb, ns, n_seg, nd).transpose(3, 0, 1, 2, 4)
-    by_layer = exchange(split, "segment", 1, n_seg, 6, False, jnp.bfloat16).sum(axis=0)
-    d_enc = exchange(by_layer, "mp", n_x * n_core, n_z, 7, False).sum(axis=0)
+    split = (
+        over_x.reshape(n_z, nb, ns, n_seg, nd).transpose(0, 3, 1, 2, 4).reshape(n_z * n_seg, nb, ns, nd)
+    )
+    d_enc = exchange(split, "mp", n_x * n_core, n_z, 6, False, jnp.bfloat16, inner="segment").sum(axis=0)
     return (context[:, None], d_enc)
 
 

time: 170 us -> 166 us (0.976)
  other arithmetic: 22.6 us -> 19 us
    select_n x4 -> x2, other arithmetic: 7.67 us -> 5.5 us  [exchange(): return jnp.where(mine, own, received)]
    pallas_call x8 -> x6, Pallas kernels: 118 us -> 119 us  [exchange(): pl.pallas_call(functools.partial(_exchange_kernel, axis, stride, count, i...]
    unnamed x29 -> x27, local copies, waits for them, and re-layouts: 5.01 us -> 5.01 us
where the time goes in v8:
time: 166 us
  Pallas kernels  119 us (72%)
  other arithmetic  19 us (11%)
  matrix products  16.2 us (10%)
  local copies, waits for them, and re-layouts  10.3 us (6%)
    pallas_call x6, Pallas kernels, exchange(): pl.pallas_call(functools.partial(_exchange_kernel, axis, stride, count, i...  119 us
    dot_general x1, matrix products, local(): jnp.einsum('btd,dh->bth', inputs, query_w, preferred_element_type=jnp.flo...  6.99 us
    select_n x2, other arithmetic, exchange(): return jnp.where(mine, own, received)  5.5 us
    dot_general x1, matrix products, local(): jnp.einsum('bzxwsch,dch->wxzbsd', grad_blocks, keyval_w, preferred_elemen...  5.28 us
    reduce_sum x1, other arithmetic, local(): exchange(layer_grad, 'mp', 1, n_core, 4, False, jnp.bfloat16).sum(axis=0)  5.1 us
    unnamed x27, local copies, waits for them, and re-layouts  5.01 us

profile of v8, /device:TPU:6, one launch (start us, length us, event | category | flops | bytes accessed | tf_op | source)
XLA Modules:
  0.0 165.7 jit_solution(7082929974029495143)
XLA Ops:
  0.6 0.0 copy-start
  0.7 0.0 copy-start.5
  0.7 0.0 copy-start.7
  0.7 0.0 copy-start.9
  0.8 0.8 iota_compare_fusion
  1.6 0.1 broadcast_in_dim.105
  1.6 0.1 broadcast_in_dim.106
  1.7 1.1 copy.47
  2.8 0.0 copy-done
  2.8 0.0 copy-start.4
  2.8 7.0 %fusion.14 = bf16[2,512,128]{1,2,0:T(8,128)(2,1)} fusion(bf16[2,1,512,4096]{3,2,1,0:T(8,128)(2,1)} %param.7, bf16[1,4096,128]{2,1,0:T(8,128)(2,1)S(1)} %copy-done), kind=kOutput, calls=%fused_computation.22 | convolution fusion | flops 1073872896 | bytes 9699328 | tf_op jit(solution)/shard_map/btd,dh->bth/dot_general | solution.py:133
  9.8 38.3 %shard_map.77 = bf16[96,2,1,8,128]{4,3,2,1,0:T(8,128)(2,1)} custom-call(bf16[2,1,8,128]{3,2,1,0:T(8,128)(2,1)} %bitcast.134), custom_call_target="tpu_custom_call" | custom-call | tf_op jit(solution)/shard_map/pallas_call | solution.py:112
  48.2 0.0 copy-done.9
  48.2 0.0 copy-done.4
  48.2 1.1 fusion.29
  49.3 0.2 broadcast_in_dim.102
  49.5 0.9 reshape_reshape.3.x_ref
  50.4 19.3 %shard_map.78 = bf16[4,6,1,8,4096]{4,3,2,1,0:T(8,128)(2,1)} custom-call(bf16[6,1,8,4096]{3,2,1,0:T(8,128)(2,1)} %reshape_reshape.3.x_ref), custom_call_target="tpu_custom_call" | custom-call | tf_op jit(solution)/shard_map/pallas_call | solution.py:112
  69.7 0.0 copy-start.2
  69.7 0.2 broadcast_in_dim.103
  69.9 1.2 copy-done.2
  71.1 1.4 bitcast_select_fusion.1.x_ref
  72.6 4.5 %shard_map.79 = bf16[2,24,1,8,4096]{4,3,2,1,0:T(8,128)(2,1)} custom-call(bf16[24,1,8,4096]{3,2,1,0:T(8,128)(2,1)} %bitcast_select_fusion.1.x_ref), custom_call_target="tpu_custom_call" | custom-call | tf_op jit(solution)/shard_map/pallas_call | solution.py:112
  77.1 0.0 copy-done.5
  77.1 0.0 copy-done.7
  77.1 0.0 copy-start.11
  77.1 4.1 %copy_select_fusion = bf16[2,4,3,2,8,4096]{5,4,0,1,2,3:T(8,128)(2,1)S(1)} fusion(bf16[2,4,3,2,8,4096]{5,4,3,2,1,0:T(8,128)(2,1)} %bitcast.112, pred[2]{0:T(512)(128)(4,1)S(1)} %iota_compare_fusion.2, pred[4]{0:T(512)(128)(4,1)S(1)} %iota_compare_fusion.1, bf16[3,2,8,4096]{3,2,1,0:T(8,128)(2,1)S(1)} %broadcast_in_dim.102, ...), kind=kLoop, calls=%fused_computation.6 | loop fusion | flops 2359296 | bytes 8257542 | tf_op jit(solution)/shard_map/jit(_where)/select_n | solution.py:125
  81.2 0.0 copy-done.11
  81.2 0.0 copy-start.3
  81.2 1.0 fusion.17
  82.2 0.1 copy.46
  82.3 0.1 copy.44
  82.5 0.0 copy-done.3
  82.5 0.7 fusion.39
  83.2 0.2 fusion.27
  83.4 0.4 fusion.21
  83.8 0.3 fusion.28
  84.0 1.6 fusion.22
  85.6 0.8 copy.58
  86.5 0.2 copy.48
  86.6 0.1 stack.7
  86.8 0.2 copy.49
  86.9 0.1 stack.8
  87.1 5.3 %bitcast_convert_fusion = (bf16[2,4,3,2,8,4096]{5,4,0,1,2,3:T(8,128)(2,1)S(1)}, f32[2,3,4,2,8,4096,1]{5,4,6,3,2,1,0:T(8,128)}) fusion(bf16[4096,2,128,1,1,1,1]{2,1,0,6,5,4,3:T(2,128)(2,1)} %bitcast.135, bf16[2,3,4,2,8,1,128]{6,4,5,3,2,1,0:T(8,128)(2,1)S(1)} %bitcast.133, bf16[2,3,4,2,8,1,128]{6,4,5,3,2,1,0:T(8,128)(2,1)S(1)} %bitcast.132), kind=kOutput, calls=%fused_computation.4 | convolution fusion | flops 806977536 | bytes 11730944 | tf_op jit(solution)/shard_map/bzxwsch,dch->wxzbsd/dot_general | solution.py:159
  92.4 2.0 %copy.53 = bf16[2,4,3,2,8,4096]{5,4,3,2,1,0:T(8,128)(2,1)} copy(bf16[2,4,3,2,8,4096]{5,4,0,1,2,3:T(8,128)(2,1)S(1)} %get-tuple-element.14) | data formatting | bytes 6291456 | tf_op jit(solution)/shard_map/convert_element_type | solution.py:110
  94.3 0.0 copy-start.8
  94.3 4.6 %shard_map.80 = bf16[2,24,1,8,4096]{4,3,2,1,0:T(8,128)(2,1)} custom-call(bf16[2,24,1,8,4096]{4,3,2,1,0:T(8,128)(2,1)} %bitcast.113), custom_call_target="tpu_custom_call" | custom-call | tf_op jit(solution)/shard_map/pallas_call | solution.py:112
  99.0 0.0 copy-done.8
  99.0 5.1 %fusion.3 = f32[4,3,2,8,4096]{4,3,0,1,2:T(8,128)S(1)} fusion(f32[2,3,4,2,8,4096,1]{5,4,6,3,2,1,0:T(8,128)} %get-tuple-element.15, pred[2]{0:T(512)(128)(4,1)S(1)} %copy-done.8, bf16[2,4,3,2,8,4096]{5,4,3,2,1,0:T(8,128)(2,1)} %bitcast.114), kind=kLoop, calls=%fused_computation.5 | loop fusion | flops 3932160 | bytes 12582914 | tf_op jit(solution)/shard_map/reduce_sum | solution.py:162
  104.1 0.2 copy.55
  104.3 0.0 copy-start.1
  104.3 1.7 %copy-done.1 = f32[4,3,2,8,4096]{4,3,2,1,0:T(8,128)} copy-done((f32[4,3,2,8,4096]{4,3,2,1,0:T(8,128)}, f32[4,3,2,8,4096]{4,3,2,1,0:T(8,128)S(1)}, u32[]{:S(2)}) %copy-start.1) | copy-done | bytes 3145752
  106.0 1.4 convert_element_type.86.x_ref
  107.3 22.3 %shard_map.81 = bf16[4,6,1,8,4096]{4,3,2,1,0:T(8,128)(2,1)} custom-call(bf16[4,6,1,8,4096]{4,3,2,1,0:T(8,128)(2,1)} %convert_element_type.86.x_ref), custom_call_target="tpu_custom_call" | custom-call | tf_op jit(solution)/shard_map/pallas_call | solution.py:112
  129.6 0.0 copy-done.6
  129.6 2.9 %select_reduce_fusion = f32[6,8,4096]{2,1,0:T(8,128)S(1)} fusion(f32[4,6,1,8,4096]{4,3,2,1,0:T(8,128)} %bitcast.110, bf16[4,6,1,8,4096]{4,3,2,1,0:T(8,128)(2,1)} %shard_map.81, pred[4]{0:T(512)(128)(4,1)S(1)} %copy-done.6), kind=kLoop, calls=%fused_computation.7 | loop fusion | flops 2162688 | bytes 5505028 | tf_op jit(solution)/shard_map/reduce_sum | solution.py:163
  132.5 0.1 copy.74
  132.7 0.1 bitcast_convert_fusion.1
  132.8 0.0 copy-start.10
  132.8 0.9 copy.56
  133.7 30.0 %shard_map.82 = bf16[96,2,1,8,128]{4,3,2,1,0:T(8,128)(2,1)} custom-call(bf16[96,2,1,8,128]{4,3,2,1,0:T(8,128)(2,1)} %bitcast.123), custom_call_target="tpu_custom_call" | custom-call | tf_op jit(solution)/shard_map/pallas_call | solution.py:112
  163.7 1.1 convert.6
  164.8 0.0 copy-done.10
  164.8 0.9 fusion.24
  (5 shorter events, 0.0 us)
Async XLA Ops:
  0.6 2.2 %copy-start = (bf16[1,4096,128]{2,1,0:T(8,128)(2,1)S(1)}, bf16[1,4096,128]{2,1,0:T(8,128)(2,1)}, u32[]{:S(2)}) copy-start(bf16[1,4096,128]{2,1,0:T(8,128)(2,1)} %param.9) | copy-start | bytes 3145732
  0.7 76.4 %copy-start.5 = (pred[4]{0:T(512)(128)(4,1)}, pred[4]{0:T(512)(128)(4,1)S(1)}, u32[]{:S(2)}) copy-start(pred[4]{0:T(512)(128)(4,1)S(1)} %iota_compare_fusion.1) | copy-start | bytes 16
  0.7 76.4 %copy-start.7 = (pred[2]{0:T(512)(128)(4,1)}, pred[2]{0:T(512)(128)(4,1)S(1)}, u32[]{:S(2)}) copy-start(pred[2]{0:T(512)(128)(4,1)S(1)} %iota_compare_fusion.2) | copy-start | bytes 10
  0.7 47.4 %copy-start.9 = (pred[3,32]{1,0:T(4,128)(4,1)}, pred[3,32]{1,0:T(4,128)(4,1)S(1)}, u32[]{:S(2)}) copy-start(pred[3,32]{1,0:T(4,128)(4,1)S(1)} %add_compare_fusion) | copy-start | bytes 292
  2.8 45.4 %copy-start.4 = (bf16[2,8,128]{2,1,0:T(8,128)(2,1)S(1)}, bf16[2,8,128]{2,1,0:T(8,128)(2,1)}, u32[]{:S(2)}) copy-start(bf16[2,8,128]{2,1,0:T(8,128)(2,1)} %param.6) | copy-start | bytes 12292
  69.7 1.4 copy-start.2
  77.1 4.1 %copy-start.11 = (bf16[1,4096,2,128]{3,2,1,0:T(2,128)(2,1)S(1)}, bf16[1,4096,2,128]{3,2,1,0:T(2,128)(2,1)}, u32[]{:S(2)}) copy-start(bf16[1,4096,2,128]{3,2,1,0:T(2,128)(2,1)} %param.10) | copy-start | bytes 6291460
  81.2 1.3 copy-start.3
  94.3 4.6 %copy-start.8 = (pred[2]{0:T(512)(128)(4,1)S(1)}, pred[2]{0:T(512)(128)(4,1)}, u32[]{:S(2)}) copy-start(pred[2]{0:T(512)(128)(4,1)} %copy-done.7) | copy-start | bytes 10
  104.3 1.7 %copy-start.1 = (f32[4,3,2,8,4096]{4,3,2,1,0:T(8,128)}, f32[4,3,2,8,4096]{4,3,2,1,0:T(8,128)S(1)}, u32[]{:S(2)}) copy-start(f32[4,3,2,8,4096]{4,3,2,1,0:T(8,128)S(1)} %copy.55) | copy-start | bytes 9437188
  107.3 22.3 %copy-start.6 = (pred[4]{0:T(512)(128)(4,1)S(1)}, pred[4]{0:T(512)(128)(4,1)}, u32[]{:S(2)}) copy-start(pred[4]{0:T(512)(128)(4,1)} %copy-done.5) | copy-start | bytes 16
  132.8 32.0 %copy-start.10 = (pred[3,32]{1,0:T(4,128)(4,1)S(1)}, pred[3,32]{1,0:T(4,128)(4,1)}, u32[]{:S(2)}) copy-start(pred[3,32]{1,0:T(4,128)(4,1)} %copy-done.9) | copy-start | bytes 292

commit v9 on v8

--- a/solution.py
+++ b/solution.py
@@ -145,19 +145,18 @@
     )
     by_x = exchange(features, "mp", n_core, n_x, 2, True)
     by_core = exchange(by_x, "mp", 1, n_core, 3, True)
-    encoder = by_core.transpose(3, 2, 1, 0, 4, 5).reshape(nb, n_mp * ns, n_seg * nd)
-    keyval = jnp.einsum(
-        "bsd,dch->bsch",
-        encoder,
-        keyval_w,
-        preferred_element_type=jnp.float32,
-    ).astype(jnp.bfloat16)
+    keyval = (
+        jnp.einsum("wxzbsd,dch->wxzbsch", by_core, keyval_w, preferred_element_type=jnp.float32)
+        .astype(jnp.bfloat16)
+        .transpose(3, 2, 1, 0, 4, 5, 6)
+        .reshape(nb, n_mp * ns, *keyval_w.shape[1:])
+    )
     total_src = keyval.shape[1]
     usable = jnp.arange(total_src)[None, :] < src_len[:, None]
     context, dkeyval = attend_pass(query, keyval, cotangent, usable)
-    grad_blocks = dkeyval.reshape(nb, n_z, n_x, n_core, ns, *dkeyval.shape[2:])
+    grad_blocks = dkeyval.reshape(nb, n_z, n_x, n_core, ns, *dkeyval.shape[2:]).transpose(3, 2, 1, 0, 4, 5, 6)
     layer_grad = jnp.einsum(
-        "bzxwsch,dch->wxzbsd", grad_blocks, keyval_w, preferred_element_type=jnp.float32
+        "wxzbsch,dch->wxzbsd", grad_blocks, keyval_w, preferred_element_type=jnp.float32
     )
     over_core = exchange(layer_grad, "mp", 1, n_core, 4, False, jnp.bfloat16).sum(axis=0)
     over_x = exchange(over_core, "mp", n_core, n_x, 5, False, jnp.bfloat16).sum(axis=0)

time: 166 us -> 168 us (1.012)
  other arithmetic: 19 us -> 21.9 us
    convert_element_type x2 -> x1, local copies, waits for them, and re-layouts: 2.87 us -> 0.89 us  [exchange(): x.astype(wire or x.dtype).reshape(lead + (pieces, -1) + tuple(block[-2:]))]
    select_n x2 -> x3, other arithmetic: 5.5 us -> 7 us  [exchange(): return jnp.where(mine, own, received)]
    unnamed x27 -> x11, local copies, waits for them, and re-layouts: 5.01 us -> 6.48 us
where the time goes in v9:
time: 168 us
  Pallas kernels  119 us (71%)
  other arithmetic  21.9 us (13%)
  matrix products  16.7 us (10%)
  local copies, waits for them, and re-layouts  9.63 us (6%)
    pallas_call x6, Pallas kernels, exchange(): pl.pallas_call(functools.partial(_exchange_kernel, axis, stride, count, i...  119 us
    select_n x3, other arithmetic, exchange(): return jnp.where(mine, own, received)  7 us
    dot_general x1, matrix products, local(): jnp.einsum('btd,dh->bth', inputs, query_w, preferred_element_type=jnp.flo...  6.51 us
    unnamed x11, local copies, waits for them, and re-layouts  6.48 us
    reduce_sum x1, other arithmetic, local(): exchange(layer_grad, 'mp', 1, n_core, 4, False, jnp.bfloat16).sum(axis=0)  5.16 us
    dot_general x1, matrix products, local(): jnp.einsum('wxzbsch,dch->wxzbsd', grad_blocks, keyval_w, preferred_elemen...  4.65 us

profile of v9, /device:TPU:6, one launch (start us, length us, event | category | flops | bytes accessed | tf_op | source)
XLA Modules:
  0.0 167.8 jit_solution(8396294679440273247)
XLA Ops:
  0.6 0.0 copy-start
  0.7 1.5 copy-done
  2.2 0.7 iota_compare_fusion
  3.0 0.1 broadcast_in_dim.103
  3.0 0.1 broadcast_in_dim.104
  3.1 1.1 copy.22
  4.2 0.0 copy-start.3
  4.2 6.5 %fusion.13 = bf16[2,512,128]{1,2,0:T(8,128)(2,1)S(1)} fusion(bf16[2,1,512,4096]{3,2,1,0:T(8,128)(2,1)} %param.7, bf16[1,4096,128]{2,1,0:T(8,128)(2,1)} %param.9), kind=kOutput, calls=%fused_computation.21 | convolution fusion | flops 1073872896 | bytes 9699328 | tf_op jit(solution)/shard_map/btd,dh->bth/dot_general | solution.py:133
  10.8 38.2 %shard_map.77 = bf16[96,2,1,8,128]{4,3,2,1,0:T(8,128)(2,1)} custom-call(bf16[2,1,8,128]{3,2,1,0:T(8,128)(2,1)} %bitcast.125), custom_call_target="tpu_custom_call" | custom-call | tf_op jit(solution)/shard_map/pallas_call | solution.py:112
  48.9 0.0 copy-done.3
  48.9 1.1 fusion.31
  50.0 0.2 broadcast_in_dim.108
  50.2 0.9 reshape_reshape.3.x_ref
  51.1 19.3 %shard_map.78 = bf16[4,6,1,8,4096]{4,3,2,1,0:T(8,128)(2,1)} custom-call(bf16[6,1,8,4096]{3,2,1,0:T(8,128)(2,1)} %reshape_reshape.3.x_ref), custom_call_target="tpu_custom_call" | custom-call | tf_op jit(solution)/shard_map/pallas_call | solution.py:112
  70.5 2.8 %bitcast_select_fusion.1 = bf16[24,8,4096]{2,1,0:T(8,128)(2,1)} fusion(bf16[4,6,1,8,4096]{4,3,2,1,0:T(8,128)(2,1)} %shard_map.78, pred[24]{0:T(512)(128)(4,1)S(1)} %broadcast_in_dim.104, bf16[3,2,8,4096]{3,2,1,0:T(8,128)(2,1)S(1)} %broadcast_in_dim.108), kind=kLoop, calls=%fused_computation.17 | loop fusion | flops 786432 | bytes 3538968 | tf_op jit(solution)/shard_map/jit(_where)/select_n | solution.py:125
  73.3 0.0 copy-start.2
  73.3 0.2 broadcast_in_dim.109
  73.4 1.2 copy-done.2
  74.7 1.5 bitcast_select_fusion.x_ref
  76.1 4.5 %shard_map.79 = bf16[2,24,1,8,4096]{4,3,2,1,0:T(8,128)(2,1)} custom-call(bf16[24,1,8,4096]{3,2,1,0:T(8,128)(2,1)} %bitcast_select_fusion.x_ref), custom_call_target="tpu_custom_call" | custom-call | tf_op jit(solution)/shard_map/pallas_call | solution.py:112
  80.6 2.7 %broadcast_select_fusion = bf16[2,24,1,8,4096]{4,3,2,1,0:T(8,128)(2,1)S(1)} fusion(bf16[2,24,1,8,4096]{4,3,2,1,0:T(8,128)(2,1)} %shard_map.79, pred[2]{0:T(512)(128)(4,1)S(1)} %iota_compare_fusion.2, bf16[24,8,4096]{2,1,0:T(8,128)(2,1)} %bitcast_select_fusion.1), kind=kLoop, calls=%fused_computation.7 | loop fusion | flops 1572864 | bytes 7864322 | tf_op jit(solution)/shard_map/jit(_where)/select_n | solution.py:125
  83.4 1.0 fusion.19
  84.5 0.1 copy.21
  84.6 0.1 copy.19
  84.7 1.8 %fusion.39 = (f32[2,2,512]{2,1,0:T(2,128)S(1)}, f32[2,2,512,192]{2,3,1,0:T(8,128)}) fusion(bf16[2,512,2,64]{1,3,2,0:T(8,128)(2,1)S(1)} %bitcast.122, bf16[2,192,2,64]{1,3,2,0:T(8,128)(2,1)S(1)} %bitcast.124, pred[2,192]{1,0:T(4,128)(4,1)S(1)} %iota_compare_fusion), kind=kOutput, calls=%fused_computation.53 | convolution fusion | flops 51904704 | bytes 1941888 | tf_op jit(solution)/shard_map/sub | solution.py:27
  86.5 1.6 fusion.29
  88.1 0.4 fusion.23
  88.5 0.3 fusion.30
  88.8 2.0 %fusion.24 = bf16[2,192,2,64]{1,3,2,0:T(8,128)(2,1)S(1)} fusion(bf16[2,512,2,64]{1,3,2,0:T(8,128)(2,1)S(1)} %bitcast.123, bf16[2,192,2,64]{1,3,2,0:T(8,128)(2,1)S(1)} %bitcast.121, bf16[2,512,2,64]{1,3,2,0:T(8,128)(2,1)S(1)} %bitcast.114, f32[2,2,512]{2,1,0:T(2,128)S(1)} %get-tuple-element.10, f32[2,2,512,192]{2,3,1,0:T(8,128)} %get-tuple-element.9, ...), kind=kOutput, calls=%fused_computation.28 | convolution fusion | flops 102678528 | bytes 2310144 | tf_op jit(solution)/shard_map/bhts,bthe->bshe/dot_general | solution.py:39
  90.8 0.8 copy.30
  91.7 0.2 copy.23
  91.8 0.1 stack.7
  92.0 0.2 copy.24
  92.2 0.1 stack.8
  92.3 4.7 %bitcast_convert_fusion = (bf16[2,4,3,2,8,4096]{5,4,3,2,1,0:T(8,128)(2,1)}, f32[2,4,3,2,8,4096,1]{5,4,6,3,2,1,0:T(8,128)}) fusion(bf16[4096,2,128,1,1,1,1]{2,1,0,6,5,4,3:T(2,128)(2,1)S(1)} %bitcast.102, bf16[2,3,4,2,8,1,128]{6,4,3,2,1,0,5:T(8,128)(2,1)S(1)} %stack.8, bf16[2,3,4,2,8,1,128]{6,4,3,2,1,0,5:T(8,128)(2,1)S(1)} %stack.7), kind=kOutput, calls=%fused_computation.5 | convolution fusion | flops 806977536 | bytes 11730944 | tf_op jit(solution)/shard_map/wxzbsch,dch->wxzbsd/dot_general | solution.py:158
  96.9 4.5 %shard_map.80 = bf16[2,24,1,8,4096]{4,3,2,1,0:T(8,128)(2,1)} custom-call(bf16[2,24,1,8,4096]{4,3,2,1,0:T(8,128)(2,1)} %bitcast.109), custom_call_target="tpu_custom_call" | custom-call | tf_op jit(solution)/shard_map/pallas_call | solution.py:112
  101.4 5.2 %fusion.3 = f32[4,3,2,8,4096]{4,3,2,1,0:T(8,128)S(1)} fusion(bf16[2,4,3,2,8,4096]{5,4,3,2,1,0:T(8,128)(2,1)} %bitcast.105, f32[2,4,3,2,8,4096,1]{5,4,6,3,2,1,0:T(8,128)} %get-tuple-element.13, pred[2]{0:T(512)(128)(4,1)S(1)} %iota_compare_fusion.2), kind=kLoop, calls=%fused_computation.4 | loop fusion | flops 3932160 | bytes 12582914 | tf_op jit(solution)/shard_map/reduce_sum | solution.py:161
  106.6 0.0 copy-start.1
  106.6 1.7 copy-done.1
  108.3 1.4 convert_element_type.91.x_ref
  109.7 22.1 %shard_map.81 = bf16[4,6,1,8,4096]{4,3,2,1,0:T(8,128)(2,1)} custom-call(bf16[4,6,1,8,4096]{4,3,2,1,0:T(8,128)(2,1)} %convert_element_type.91.x_ref), custom_call_target="tpu_custom_call" | custom-call | tf_op jit(solution)/shard_map/pallas_call | solution.py:112
  131.8 2.9 %select_reduce_fusion = f32[6,8,4096]{2,1,0:T(8,128)S(1)} fusion(f32[4,6,1,8,4096]{4,3,2,1,0:T(8,128)} %bitcast.104, bf16[4,6,1,8,4096]{4,3,2,1,0:T(8,128)(2,1)} %shard_map.81, pred[4]{0:T(512)(128)(4,1)S(1)} %iota_compare_fusion.1), kind=kLoop, calls=%fused_computation.6 | loop fusion | flops 2162688 | bytes 5505028 | tf_op jit(solution)/shard_map/reduce_sum | solution.py:162
  134.7 0.1 copy.50
  134.8 0.1 bitcast_convert_fusion.1
  134.9 0.9 copy.28
  135.8 30.1 %shard_map.82 = bf16[96,2,1,8,128]{4,3,2,1,0:T(8,128)(2,1)} custom-call(bf16[96,2,1,8,128]{4,3,2,1,0:T(8,128)(2,1)} %bitcast.115), custom_call_target="tpu_custom_call" | custom-call | tf_op jit(solution)/shard_map/pallas_call | solution.py:112
  165.9 1.1 convert.6
  166.9 0.9 fusion.26
  (5 shorter events, 0.1 us)
Async XLA Ops:
  0.6 1.6 copy-start
  4.2 44.7 %copy-start.3 = (bf16[2,8,128]{2,1,0:T(8,128)(2,1)S(1)}, bf16[2,8,128]{2,1,0:T(8,128)(2,1)}, u32[]{:S(2)}) copy-start(bf16[2,8,128]{2,1,0:T(8,128)(2,1)} %param.6) | copy-start | bytes 12292
  73.3 1.4 copy-start.2
  106.6 1.7 copy-start.1

commit v10 on v8

--- a/solution.py
+++ b/solution.py
@@ -161,10 +161,9 @@
     )
     over_core = exchange(layer_grad, "mp", 1, n_core, 4, False, jnp.bfloat16).sum(axis=0)
     over_x = exchange(over_core, "mp", n_core, n_x, 5, False, jnp.bfloat16).sum(axis=0)
-    split = (
-        over_x.reshape(n_z, nb, ns, n_seg, nd).transpose(0, 3, 1, 2, 4).reshape(n_z * n_seg, nb, ns, nd)
-    )
-    d_enc = exchange(split, "mp", n_x * n_core, n_z, 6, False, jnp.bfloat16, inner="segment").sum(axis=0)
+    split = over_x.reshape(n_z, nb, ns, n_seg, nd).transpose(3, 0, 1, 2, 4)
+    by_layer = exchange(split, "segment", 1, n_seg, 6, False, jnp.bfloat16).sum(axis=0)
+    d_enc = exchange(by_layer, "mp", n_x * n_core, n_z, 7, False).sum(axis=0)
     return (context[:, None], d_enc)
 
 

time: 166 us -> 170 us (1.024)
  other arithmetic: 19 us -> 23.5 us
    select_n x2 -> x3, other arithmetic: 5.5 us -> 7.41 us  [exchange(): return jnp.where(mine, own, received)]
    pallas_call x6 -> x7, Pallas kernels: 119 us -> 120 us  [exchange(): pl.pallas_call(functools.partial(_exchange_kernel, axis, stride, count, i...]
where the time goes in v10:
time: 170 us
  Pallas kernels  120 us (71%)
  other arithmetic  23.5 us (14%)
  matrix products  16.2 us (10%)
  local copies, waits for them, and re-layouts  9.23 us (5%)
    pallas_call x7, Pallas kernels, exchange(): pl.pallas_call(functools.partial(_exchange_kernel, axis, stride, count, i...  120 us
    select_n x3, other arithmetic, exchange(): return jnp.where(mine, own, received)  7.41 us
    dot_general x1, matrix products, local(): jnp.einsum('btd,dh->bth', inputs, query_w, preferred_element_type=jnp.flo...  6.99 us
    dot_general x1, matrix products, local(): jnp.einsum('bzxwsch,dch->wxzbsd', grad_blocks, keyval_w, preferred_elemen...  5.28 us
    reduce_sum x1, other arithmetic, local(): exchange(layer_grad, 'mp', 1, n_core, 4, False, jnp.bfloat16).sum(axis=0)  5.1 us
    unnamed x27, local copies, waits for them, and re-layouts  5.01 us

profile of v10, /device:TPU:6, one launch (start us, length us, event | category | flops | bytes accessed | tf_op | source)
XLA Modules:
  0.0 169.8 jit_solution(9199836853627309101)
XLA Ops:
  0.6 0.0 copy-start
  0.7 0.0 copy-start.5
  0.7 0.0 copy-start.7
  0.8 0.5 iota_compare_fusion.2
  1.3 0.6 iota_compare_fusion.1
  1.9 0.7 iota_compare_fusion
  2.6 0.1 broadcast_in_dim.115
  2.7 0.1 broadcast_in_dim.116
  2.8 1.1 copy.47
  3.9 0.0 copy-done
  3.9 0.0 copy-start.4
  3.9 7.0 %fusion.14 = bf16[2,512,128]{1,2,0:T(8,128)(2,1)} fusion(bf16[2,1,512,4096]{3,2,1,0:T(8,128)(2,1)} %param.7, bf16[1,4096,128]{2,1,0:T(8,128)(2,1)S(1)} %copy-done), kind=kOutput, calls=%fused_computation.22 | convolution fusion | flops 1073872896 | bytes 9699328 | tf_op jit(solution)/shard_map/btd,dh->bth/dot_general | solution.py:133
  10.9 38.4 %shard_map.77 = bf16[96,2,1,8,128]{4,3,2,1,0:T(8,128)(2,1)} custom-call(bf16[2,1,8,128]{3,2,1,0:T(8,128)(2,1)} %bitcast.144), custom_call_target="tpu_custom_call" | custom-call | tf_op jit(solution)/shard_map/pallas_call | solution.py:112
  49.2 0.0 copy-done.4
  49.3 1.2 fusion.50
  50.4 1.9 %copy_select_fusion.1 = bf16[3,32,2,8,128]{4,3,1,2,0:T(8,128)(2,1)} fusion(bf16[3,32,2,8,128]{4,3,2,1,0:T(8,128)(2,1)} %bitcast.126, pred[3,32]{1,0:T(4,128)(4,1)S(1)} %add_compare_fusion, bf16[2,8,128]{2,1,0:T(8,128)(2,1)S(1)} %copy-done.4), kind=kLoop, calls=%fused_computation.40 | loop fusion | flops 196608 | bytes 790624 | tf_op jit(solution)/shard_map/jit(_where)/select_n | solution.py:125
  52.3 19.3 %shard_map.78 = bf16[4,6,1,8,4096]{4,3,2,1,0:T(8,128)(2,1)} custom-call(bf16[6,1,8,4096]{3,2,1,0:T(8,128)(2,1)} %bitcast.134), custom_call_target="tpu_custom_call" | custom-call | tf_op jit(solution)/shard_map/pallas_call | solution.py:112
  71.7 0.0 copy-start.2
  71.7 0.2 broadcast_in_dim.113
  71.9 1.2 copy-done.2
  73.1 1.4 bitcast_select_fusion.1.x_ref
  74.5 4.5 %shard_map.79 = bf16[2,24,1,8,4096]{4,3,2,1,0:T(8,128)(2,1)} custom-call(bf16[24,1,8,4096]{3,2,1,0:T(8,128)(2,1)} %bitcast_select_fusion.1.x_ref), custom_call_target="tpu_custom_call" | custom-call | tf_op jit(solution)/shard_map/pallas_call | solution.py:112
  79.0 0.0 copy-done.5
  79.0 0.0 copy-done.7
  79.0 0.0 copy-start.11
  79.1 4.1 %copy_select_fusion = bf16[2,4,3,2,8,4096]{5,4,0,1,2,3:T(8,128)(2,1)S(1)} fusion(bf16[2,4,3,2,8,4096]{5,4,3,2,1,0:T(8,128)(2,1)} %bitcast.119, pred[2]{0:T(512)(128)(4,1)S(1)} %iota_compare_fusion.4, pred[4]{0:T(512)(128)(4,1)S(1)} %iota_compare_fusion.3, bf16[3,2,8,4096]{3,2,1,0:T(8,128)(2,1)S(1)} %fusion.50, bf16[4,3,2,8,4096]{4,3,2,1,0:T(8,128)(2,1)S(1)} %bitcast.118), kind=kLoop, calls=%fused_computation.6 | loop fusion | flops 2359296 | bytes 8257542 | tf_op jit(solution)/shard_map/jit(_where)/select_n | solution.py:125
  83.1 0.0 copy-done.11
  83.1 0.0 copy-start.3
  83.1 1.0 fusion.17
  84.2 0.1 copy.46
  84.3 0.1 copy.44
  84.4 0.0 copy-done.3
  84.4 0.7 fusion.39
  85.1 0.2 fusion.27
  85.3 0.4 fusion.21
  85.7 0.3 fusion.28
  86.0 1.6 fusion.22
  87.6 0.8 copy.58
  88.4 0.2 copy.48
  88.6 0.1 stack.7
  88.7 0.2 copy.49
  88.9 0.1 stack.8
  89.0 5.3 %bitcast_convert_fusion = (bf16[2,4,3,2,8,4096]{5,4,0,1,2,3:T(8,128)(2,1)S(1)}, f32[2,3,4,2,8,4096,1]{5,4,6,3,2,1,0:T(8,128)}) fusion(bf16[4096,2,128,1,1,1,1]{2,1,0,6,5,4,3:T(2,128)(2,1)} %bitcast.145, bf16[2,3,4,2,8,1,128]{6,4,5,3,2,1,0:T(8,128)(2,1)S(1)} %bitcast.143, bf16[2,3,4,2,8,1,128]{6,4,5,3,2,1,0:T(8,128)(2,1)S(1)} %bitcast.142), kind=kOutput, calls=%fused_computation.4 | convolution fusion | flops 806977536 | bytes 11730944 | tf_op jit(solution)/shard_map/bzxwsch,dch->wxzbsd/dot_general | solution.py:159
  94.3 2.0 %copy.53 = bf16[2,4,3,2,8,4096]{5,4,3,2,1,0:T(8,128)(2,1)} copy(bf16[2,4,3,2,8,4096]{5,4,0,1,2,3:T(8,128)(2,1)S(1)} %get-tuple-element.14) | data formatting | bytes 6291456 | tf_op jit(solution)/shard_map/convert_element_type | solution.py:110
  96.3 4.6 %shard_map.80 = bf16[2,24,1,8,4096]{4,3,2,1,0:T(8,128)(2,1)} custom-call(bf16[2,24,1,8,4096]{4,3,2,1,0:T(8,128)(2,1)} %bitcast.120), custom_call_target="tpu_custom_call" | custom-call | tf_op jit(solution)/shard_map/pallas_call | solution.py:112
  100.9 0.0 copy-done.8
  100.9 5.1 %fusion.3 = f32[4,3,2,8,4096]{4,3,0,1,2:T(8,128)S(1)} fusion(f32[2,3,4,2,8,4096,1]{5,4,6,3,2,1,0:T(8,128)} %get-tuple-element.15, pred[2]{0:T(512)(128)(4,1)S(1)} %copy-done.8, bf16[2,4,3,2,8,4096]{5,4,3,2,1,0:T(8,128)(2,1)} %bitcast.121), kind=kLoop, calls=%fused_computation.5 | loop fusion | flops 3932160 | bytes 12582914 | tf_op jit(solution)/shard_map/reduce_sum | solution.py:162
  106.0 0.2 copy.55
  106.2 0.0 copy-start.1
  106.3 1.7 copy-done.1
  107.9 1.4 convert_element_type.75.x_ref
  109.3 22.3 %shard_map.81 = bf16[4,6,1,8,4096]{4,3,2,1,0:T(8,128)(2,1)} custom-call(bf16[4,6,1,8,4096]{4,3,2,1,0:T(8,128)(2,1)} %convert_element_type.75.x_ref), custom_call_target="tpu_custom_call" | custom-call | tf_op jit(solution)/shard_map/pallas_call | solution.py:112
  131.6 0.0 copy-done.6
  131.6 2.9 %select_reduce_fusion = f32[6,8,4096]{2,1,0:T(8,128)S(1)} fusion(f32[4,6,1,8,4096]{4,3,2,1,0:T(8,128)} %bitcast.117, bf16[4,6,1,8,4096]{4,3,2,1,0:T(8,128)(2,1)} %shard_map.81, pred[4]{0:T(512)(128)(4,1)S(1)} %copy-done.6), kind=kLoop, calls=%fused_computation.7 | loop fusion | flops 2162688 | bytes 5505028 | tf_op jit(solution)/shard_map/reduce_sum | solution.py:163
  134.5 0.1 copy.74
  134.6 0.1 bitcast_convert_fusion.1
  134.7 0.0 copy-start.10
  134.7 0.9 copy.56
  135.6 22.0 %shard_map.82 = bf16[32,6,1,8,128]{4,3,2,1,0:T(8,128)(2,1)} custom-call(bf16[32,6,1,8,128]{4,3,2,1,0:T(8,128)(2,1)} %bitcast.132), custom_call_target="tpu_custom_call" | custom-call | tf_op jit(solution)/shard_map/pallas_call | solution.py:112
  157.6 0.0 copy-start.9
  157.6 1.0 bitcast_convert_fusion.2
  158.7 1.0 fusion.24
  159.6 8.7 %shard_map.83 = f32[3,2,1,8,128]{4,3,2,1,0:T(8,128)} custom-call(f32[3,2,1,8,128]{4,3,2,1,0:T(8,128)} %bitcast.140), custom_call_target="tpu_custom_call" | custom-call | tf_op jit(solution)/shard_map/pallas_call | solution.py:112
  168.3 1.4 fusion.32
  (8 shorter events, 0.0 us)
Async XLA Ops:
  0.6 3.2 %copy-start = (bf16[1,4096,128]{2,1,0:T(8,128)(2,1)S(1)}, bf16[1,4096,128]{2,1,0:T(8,128)(2,1)}, u32[]{:S(2)}) copy-start(bf16[1,4096,128]{2,1,0:T(8,128)(2,1)} %param.9) | copy-start | bytes 3145732
  0.7 78.3 %copy-start.5 = (pred[4]{0:T(512)(128)(4,1)}, pred[4]{0:T(512)(128)(4,1)S(1)}, u32[]{:S(2)}) copy-start(pred[4]{0:T(512)(128)(4,1)S(1)} %iota_compare_fusion.3) | copy-start | bytes 16
  0.7 78.3 %copy-start.7 = (pred[2]{0:T(512)(128)(4,1)}, pred[2]{0:T(512)(128)(4,1)S(1)}, u32[]{:S(2)}) copy-start(pred[2]{0:T(512)(128)(4,1)S(1)} %iota_compare_fusion.4) | copy-start | bytes 10
  3.9 45.4 %copy-start.4 = (bf16[2,8,128]{2,1,0:T(8,128)(2,1)S(1)}, bf16[2,8,128]{2,1,0:T(8,128)(2,1)}, u32[]{:S(2)}) copy-start(bf16[2,8,128]{2,1,0:T(8,128)(2,1)} %param.6) | copy-start | bytes 12292
  71.7 1.4 copy-start.2
  79.0 4.1 %copy-start.11 = (bf16[1,4096,2,128]{3,2,1,0:T(2,128)(2,1)S(1)}, bf16[1,4096,2,128]{3,2,1,0:T(2,128)(2,1)}, u32[]{:S(2)}) copy-start(bf16[1,4096,2,128]{3,2,1,0:T(2,128)(2,1)} %param.10) | copy-start | bytes 6291460
  83.1 1.3 copy-start.3
  96.3 4.6 %copy-start.8 = (pred[2]{0:T(512)(128)(4,1)S(1)}, pred[2]{0:T(512)(128)(4,1)}, u32[]{:S(2)}) copy-start(pred[2]{0:T(512)(128)(4,1)} %copy-done.7) | copy-start | bytes 10
  106.2 1.7 copy-start.1
  109.3 22.3 %copy-start.6 = (pred[4]{0:T(512)(128)(4,1)S(1)}, pred[4]{0:T(512)(128)(4,1)}, u32[]{:S(2)}) copy-start(pred[4]{0:T(512)(128)(4,1)} %copy-done.5) | copy-start | bytes 16
  134.7 24.0 %copy-start.10 = (pred[32]{0:T(512)(128)(4,1)S(1)}, pred[32]{0:T(512)(128)(4,1)}, u32[]{:S(2)}) copy-start(pred[32]{0:T(512)(128)(4,1)} %iota_compare_fusion.1) | copy-start | bytes 100
  157.6 10.7 %copy-start.9 = (pred[3]{0:T(512)(128)(4,1)S(1)}, pred[3]{0:T(512)(128)(4,1)}, u32[]{:S(2)}) copy-start(pred[3]{0:T(512)(128)(4,1)} %iota_compare_fusion.2) | copy-start | bytes 13

commit v11 on v8

--- a/solution.py
+++ b/solution.py
@@ -75,7 +75,7 @@
     pl.semaphore_wait(barrier, total - 1)
 
     def send(i, carry):
-        k = 1 + lax.div(i, pieces)
+        k = 1 + lax.rem(lax.div(i, pieces) + n_inner - 1, total - 1)
         p = lax.rem(i, pieces)
         slot = lax.rem(mine + k, total)
         block = x_ref.at[p] if gather else x_ref.at[slot, p]

time: 166 us -> 166 us (level)
  no operation moved by 1% of the time
where the time goes in v11:
time: 166 us; the launch traced here: 165 us
  Pallas kernels  119 us (72%)
  other arithmetic  19 us (11%)
  matrix products  16.2 us (10%)
  local copies, waits for them, and re-layouts  10.3 us (6%)
    pallas_call x6, Pallas kernels, exchange(): pl.pallas_call(functools.partial(_exchange_kernel, axis, stride, count, i...  119 us
    dot_general x1, matrix products, local(): jnp.einsum('btd,dh->bth', inputs, query_w, preferred_element_type=jnp.flo...  6.99 us
    select_n x2, other arithmetic, exchange(): return jnp.where(mine, own, received)  5.5 us
    dot_general x1, matrix products, local(): jnp.einsum('bzxwsch,dch->wxzbsd', grad_blocks, keyval_w, preferred_elemen...  5.27 us
    reduce_sum x1, other arithmetic, local(): exchange(layer_grad, 'mp', 1, n_core, 4, False, jnp.bfloat16).sum(axis=0)  5.1 us
    unnamed x27, local copies, waits for them, and re-layouts  5.01 us

profile of v11, /device:TPU:6, one launch (start us, length us, event | category | flops | bytes accessed | tf_op | source)
XLA Modules:
  0.0 165.3 jit_solution(2178721938082229439)
XLA Ops:
  0.6 0.0 copy-start
  0.7 0.0 copy-start.5
  0.7 0.0 copy-start.7
  0.7 0.0 copy-start.9
  0.8 0.8 iota_compare_fusion
  1.6 0.1 broadcast_in_dim.105
  1.6 0.1 broadcast_in_dim.106
  1.7 1.1 copy.47
  2.8 0.0 copy-done
  2.8 0.0 copy-start.4
  2.8 7.0 %fusion.14 = bf16[2,512,128]{1,2,0:T(8,128)(2,1)} fusion(bf16[2,1,512,4096]{3,2,1,0:T(8,128)(2,1)} %param.7, bf16[1,4096,128]{2,1,0:T(8,128)(2,1)S(1)} %copy-done), kind=kOutput, calls=%fused_computation.22 | convolution fusion | flops 1073872896 | bytes 9699328 | tf_op jit(solution)/shard_map/btd,dh->bth/dot_general | solution.py:133
  9.8 36.4 %shard_map.77 = bf16[96,2,1,8,128]{4,3,2,1,0:T(8,128)(2,1)} custom-call(bf16[2,1,8,128]{3,2,1,0:T(8,128)(2,1)} %bitcast.134), custom_call_target="tpu_custom_call" | custom-call | tf_op jit(solution)/shard_map/pallas_call | solution.py:112
  46.2 0.0 copy-done.9
  46.3 0.0 copy-done.4
  46.3 1.1 fusion.29
  47.4 0.2 broadcast_in_dim.102
  47.5 0.9 reshape_reshape.3.x_ref
  48.5 19.9 %shard_map.78 = bf16[4,6,1,8,4096]{4,3,2,1,0:T(8,128)(2,1)} custom-call(bf16[6,1,8,4096]{3,2,1,0:T(8,128)(2,1)} %reshape_reshape.3.x_ref), custom_call_target="tpu_custom_call" | custom-call | tf_op jit(solution)/shard_map/pallas_call | solution.py:112
  68.4 0.0 copy-start.2
  68.4 0.2 broadcast_in_dim.103
  68.6 1.2 copy-done.2
  69.8 1.4 bitcast_select_fusion.1.x_ref
  71.3 4.5 %shard_map.79 = bf16[2,24,1,8,4096]{4,3,2,1,0:T(8,128)(2,1)} custom-call(bf16[24,1,8,4096]{3,2,1,0:T(8,128)(2,1)} %bitcast_select_fusion.1.x_ref), custom_call_target="tpu_custom_call" | custom-call | tf_op jit(solution)/shard_map/pallas_call | solution.py:112
  75.8 0.0 copy-done.5
  75.8 0.0 copy-done.7
  75.8 0.0 copy-start.11
  75.8 4.1 %copy_select_fusion = bf16[2,4,3,2,8,4096]{5,4,0,1,2,3:T(8,128)(2,1)S(1)} fusion(bf16[2,4,3,2,8,4096]{5,4,3,2,1,0:T(8,128)(2,1)} %bitcast.112, pred[2]{0:T(512)(128)(4,1)S(1)} %iota_compare_fusion.2, pred[4]{0:T(512)(128)(4,1)S(1)} %iota_compare_fusion.1, bf16[3,2,8,4096]{3,2,1,0:T(8,128)(2,1)S(1)} %broadcast_in_dim.102, ...), kind=kLoop, calls=%fused_computation.6 | loop fusion | flops 2359296 | bytes 8257542 | tf_op jit(solution)/shard_map/jit(_where)/select_n | solution.py:125
  79.9 0.0 copy-done.11
  79.9 0.0 copy-start.3
  79.9 1.0 fusion.17
  80.9 0.1 copy.46
  81.0 0.1 copy.44
  81.1 0.0 copy-done.3
  81.1 0.7 fusion.39
  81.8 0.2 fusion.27
  82.1 0.4 fusion.21
  82.4 0.3 fusion.28
  82.7 1.6 fusion.22
  84.3 0.8 copy.58
  85.1 0.2 copy.48
  85.3 0.1 stack.7
  85.4 0.2 copy.49
  85.6 0.1 stack.8
  85.7 5.3 %bitcast_convert_fusion = (bf16[2,4,3,2,8,4096]{5,4,0,1,2,3:T(8,128)(2,1)S(1)}, f32[2,3,4,2,8,4096,1]{5,4,6,3,2,1,0:T(8,128)}) fusion(bf16[4096,2,128,1,1,1,1]{2,1,0,6,5,4,3:T(2,128)(2,1)} %bitcast.135, bf16[2,3,4,2,8,1,128]{6,4,5,3,2,1,0:T(8,128)(2,1)S(1)} %bitcast.133, bf16[2,3,4,2,8,1,128]{6,4,5,3,2,1,0:T(8,128)(2,1)S(1)} %bitcast.132), kind=kOutput, calls=%fused_computation.4 | convolution fusion | flops 806977536 | bytes 11730944 | tf_op jit(solution)/shard_map/bzxwsch,dch->wxzbsd/dot_general | solution.py:159
  91.0 2.0 %copy.53 = bf16[2,4,3,2,8,4096]{5,4,3,2,1,0:T(8,128)(2,1)} copy(bf16[2,4,3,2,8,4096]{5,4,0,1,2,3:T(8,128)(2,1)S(1)} %get-tuple-element.14) | data formatting | bytes 6291456 | tf_op jit(solution)/shard_map/convert_element_type | solution.py:110
  93.0 0.0 copy-start.8
  93.0 4.6 %shard_map.80 = bf16[2,24,1,8,4096]{4,3,2,1,0:T(8,128)(2,1)} custom-call(bf16[2,24,1,8,4096]{4,3,2,1,0:T(8,128)(2,1)} %bitcast.113), custom_call_target="tpu_custom_call" | custom-call | tf_op jit(solution)/shard_map/pallas_call | solution.py:112
  97.6 0.0 copy-done.8
  97.6 5.1 %fusion.3 = f32[4,3,2,8,4096]{4,3,0,1,2:T(8,128)S(1)} fusion(f32[2,3,4,2,8,4096,1]{5,4,6,3,2,1,0:T(8,128)} %get-tuple-element.15, pred[2]{0:T(512)(128)(4,1)S(1)} %copy-done.8, bf16[2,4,3,2,8,4096]{5,4,3,2,1,0:T(8,128)(2,1)} %bitcast.114), kind=kLoop, calls=%fused_computation.5 | loop fusion | flops 3932160 | bytes 12582914 | tf_op jit(solution)/shard_map/reduce_sum | solution.py:162
  102.8 0.2 copy.55
  103.0 0.0 copy-start.1
  103.0 1.7 %copy-done.1 = f32[4,3,2,8,4096]{4,3,2,1,0:T(8,128)} copy-done((f32[4,3,2,8,4096]{4,3,2,1,0:T(8,128)}, f32[4,3,2,8,4096]{4,3,2,1,0:T(8,128)S(1)}, u32[]{:S(2)}) %copy-start.1) | copy-done | bytes 3145752
  104.6 1.4 convert_element_type.86.x_ref
  106.0 22.3 %shard_map.81 = bf16[4,6,1,8,4096]{4,3,2,1,0:T(8,128)(2,1)} custom-call(bf16[4,6,1,8,4096]{4,3,2,1,0:T(8,128)(2,1)} %convert_element_type.86.x_ref), custom_call_target="tpu_custom_call" | custom-call | tf_op jit(solution)/shard_map/pallas_call | solution.py:112
  128.3 0.0 copy-done.6
  128.3 2.9 %select_reduce_fusion = f32[6,8,4096]{2,1,0:T(8,128)S(1)} fusion(f32[4,6,1,8,4096]{4,3,2,1,0:T(8,128)} %bitcast.110, bf16[4,6,1,8,4096]{4,3,2,1,0:T(8,128)(2,1)} %shard_map.81, pred[4]{0:T(512)(128)(4,1)S(1)} %copy-done.6), kind=kLoop, calls=%fused_computation.7 | loop fusion | flops 2162688 | bytes 5505028 | tf_op jit(solution)/shard_map/reduce_sum | solution.py:163
  131.2 0.1 copy.74
  131.3 0.1 bitcast_convert_fusion.1
  131.4 0.0 copy-start.10
  131.4 0.9 copy.56
  132.3 31.0 %shard_map.82 = bf16[96,2,1,8,128]{4,3,2,1,0:T(8,128)(2,1)} custom-call(bf16[96,2,1,8,128]{4,3,2,1,0:T(8,128)(2,1)} %bitcast.123), custom_call_target="tpu_custom_call" | custom-call | tf_op jit(solution)/shard_map/pallas_call | solution.py:112
  163.3 1.1 convert.6
  164.4 0.0 copy-done.10
  164.4 0.9 fusion.24
  (5 shorter events, 0.0 us)
Async XLA Ops:
  0.6 2.2 %copy-start = (bf16[1,4096,128]{2,1,0:T(8,128)(2,1)S(1)}, bf16[1,4096,128]{2,1,0:T(8,128)(2,1)}, u32[]{:S(2)}) copy-start(bf16[1,4096,128]{2,1,0:T(8,128)(2,1)} %param.9) | copy-start | bytes 3145732
  0.7 75.1 %copy-start.5 = (pred[4]{0:T(512)(128)(4,1)}, pred[4]{0:T(512)(128)(4,1)S(1)}, u32[]{:S(2)}) copy-start(pred[4]{0:T(512)(128)(4,1)S(1)} %iota_compare_fusion.1) | copy-start | bytes 16
  0.7 75.1 %copy-start.7 = (pred[2]{0:T(512)(128)(4,1)}, pred[2]{0:T(512)(128)(4,1)S(1)}, u32[]{:S(2)}) copy-start(pred[2]{0:T(512)(128)(4,1)S(1)} %iota_compare_fusion.2) | copy-start | bytes 10
  0.7 45.5 %copy-start.9 = (pred[3,32]{1,0:T(4,128)(4,1)}, pred[3,32]{1,0:T(4,128)(4,1)S(1)}, u32[]{:S(2)}) copy-start(pred[3,32]{1,0:T(4,128)(4,1)S(1)} %add_compare_fusion) | copy-start | bytes 292
  2.8 43.4 %copy-start.4 = (bf16[2,8,128]{2,1,0:T(8,128)(2,1)S(1)}, bf16[2,8,128]{2,1,0:T(8,128)(2,1)}, u32[]{:S(2)}) copy-start(bf16[2,8,128]{2,1,0:T(8,128)(2,1)} %param.6) | copy-start | bytes 12292
  68.4 1.4 copy-start.2
  75.8 4.1 %copy-start.11 = (bf16[1,4096,2,128]{3,2,1,0:T(2,128)(2,1)S(1)}, bf16[1,4096,2,128]{3,2,1,0:T(2,128)(2,1)}, u32[]{:S(2)}) copy-start(bf16[1,4096,2,128]{3,2,1,0:T(2,128)(2,1)} %param.10) | copy-start | bytes 6291460
  79.9 1.3 copy-start.3
  93.0 4.6 %copy-start.8 = (pred[2]{0:T(512)(128)(4,1)S(1)}, pred[2]{0:T(512)(128)(4,1)}, u32[]{:S(2)}) copy-start(pred[2]{0:T(512)(128)(4,1)} %copy-done.7) | copy-start | bytes 10
  103.0 1.7 %copy-start.1 = (f32[4,3,2,8,4096]{4,3,2,1,0:T(8,128)}, f32[4,3,2,8,4096]{4,3,2,1,0:T(8,128)S(1)}, u32[]{:S(2)}) copy-start(f32[4,3,2,8,4096]{4,3,2,1,0:T(8,128)S(1)} %copy.55) | copy-start | bytes 9437188
  106.0 22.3 %copy-start.6 = (pred[4]{0:T(512)(128)(4,1)S(1)}, pred[4]{0:T(512)(128)(4,1)}, u32[]{:S(2)}) copy-start(pred[4]{0:T(512)(128)(4,1)} %copy-done.5) | copy-start | bytes 16
  131.4 33.0 %copy-start.10 = (pred[3,32]{1,0:T(4,128)(4,1)S(1)}, pred[3,32]{1,0:T(4,128)(4,1)}, u32[]{:S(2)}) copy-start(pred[3,32]{1,0:T(4,128)(4,1)} %copy-done.9) | copy-start | bytes 292
